TPU v7x, 32 devices: a whole 2x2x4 slice. The times are simulated.
32 devices in a mesh: dp: 8 (over y, x, core), mp: 4 (over z).
Axes of the slice: x: 2, y: 2, z: 4, core: 2. Of those that a mesh axis runs over, the one named last changes fastest.
Arguments:
- tokens: bfloat16 [8192, 640], P(('dp', 'mp')), may hold values from -6 to 6
- lengths: int32 [8], P('dp'), may hold values from 20 to 1024, as said below
- key_keep: int32 [8, 1024], P('dp'), may hold values 0 or 1
- ln_gain: float32 [2, 2, 640], replicated, may hold values from 0.25 to 1.75
- ln_bias: float32 [2, 2, 640], replicated, may hold values from -1.5 to 1.5
- w_qkv: bfloat16 [2, 640, 3, 640], P(None, None, None, 'mp'), may hold values from -0.25 to 0.25
- w_out: bfloat16 [2, 640, 640], P(None, 'mp'), may hold values from -1 to 1
- w_up: bfloat16 [2, 640, 5120], P(None, None, 'mp'), may hold values from -0.25 to 0.25
- w_down: bfloat16 [2, 5120, 640], P(None, 'mp'), may hold values from -0.078125 to 0.078125
- readout: bfloat16 [640, 25], replicated, may hold values from -0.5 to 0.5
- labels: int32 [8192], P(('dp', 'mp')), may hold values from 0 to 24
- cotangent: bfloat16 [8192, 640], P(('dp', 'mp')), may hold values from -6 to 6
Outputs:
- layer_out: bfloat16 [8192, 640], P(('dp', 'mp'))
- grad_tokens: float32 [8192, 640], P(('dp', 'mp'))
- grad_ln_gain: float32 [2, 2, 640], replicated
- grad_ln_bias: float32 [2, 2, 640], replicated
- grad_w_qkv: float32 [2, 640, 3, 640], P(None, None, None, 'mp')
- grad_w_out: float32 [2, 640, 640], P(None, 'mp')
- grad_w_up: float32 [2, 640, 5120], P(None, None, 'mp')
- grad_w_down: float32 [2, 5120, 640], P(None, 'mp')
- label_logprob: float32 [8192], P(('dp', 'mp'))
- token_count: int32 [], replicated
Inputs may be any that keep to these rules, and one draw needn't show every extreme that they name: `lengths`: each sequence's true length; in every draw some sequence has length exactly 1024.
All inputs are finite; a program needn't handle non-finite values. No bound on the sum of `key_keep` on one device may be relied on, other than what follows from the above.
Results may differ from a plain program's by a relative error of at most 0.017.
Values may be sent and summed in bfloat16 or wider, within the bound.
No kernel may reach another device: no remote copies, remote signals or barrier semaphores. Data moves between devices by JAX's collectives and lax.ppermute only.
A program may use at most 192 MiB of HBM per device.

v0:
```python
import functools
import math

import jax
import jax.numpy as jnp
from jax import lax
from jax.experimental import pallas as pl
from jax.experimental.pallas import tpu as pltpu
from jax.sharding import Mesh, PartitionSpec as P

HD = 32
LAYERS = 2


EPS = 1e-05
NEG = -1000000000.0
ROOT_HALF = 0.7071067811865476
INV_ROOT_TAU = 0.3989422804014327
LOG2_E = 1.4426950408889634
VMEM_LIMIT = 56 * 1024 * 1024

BF = jnp.bfloat16
F32 = jnp.float32
FLIP = [(0, 1), (1, 0)]

HOME = []
for _c in range(2):
    for _h in range(2):
        for _p in range(2):
            _to = (_c, _h, _p) if _c == _h else (1 - _c, 1 - _h, _p)
            HOME.append((4 * _c + 2 * _h + _p, 4 * _to[0] + 2 * _to[1] + _to[2]))


def rehome(x):
    return lax.ppermute(x, ("c", "zh", "zl"), HOME)


def flip(x, axis):
    return lax.ppermute(x, axis, FLIP)


def tie(x, *before):
    return lax.optimization_barrier((x, before))[0]


def whole(*shape):
    return pl.BlockSpec(shape, lambda *_: (0,) * len(shape))


def kernel_params(micros):
    return dict(
        compiler_params=pltpu.CompilerParams(vmem_limit_bytes=VMEM_LIMIT),
        cost_estimate=pl.CostEstimate(
            flops=int(micros * 1.15e9), bytes_accessed=1 << 20, transcendentals=0
        ),
    )


def norm_unit(values):
    mean = jnp.mean(values, axis=-1, keepdims=True)
    centred = values - mean
    spread = jnp.mean(centred * centred, axis=-1, keepdims=True)
    inverse = lax.rsqrt(spread + EPS)
    return centred * inverse, inverse


def norm_forward_kernel(count, hidden_ref, *refs):
    parts = refs[:count]
    gain_ref, bias_ref, sum_ref, normed_ref = refs[count:]
    values = hidden_ref[...].astype(F32)
    for part in parts:
        values = values + part[...].astype(F32)
    sum_ref[...] = values
    unit, _ = norm_unit(values)
    normed_ref[...] = (unit * gain_ref[...] + bias_ref[...]).astype(BF)


def norm_forward(hidden, parts, gain, bias):
    rows, model = hidden.shape
    return pl.pallas_call(
        functools.partial(norm_forward_kernel, len(parts)),
        out_shape=[
            jax.ShapeDtypeStruct((rows, model), F32),
            jax.ShapeDtypeStruct((rows, model), BF),
        ],
        name="norm_forward",
        **kernel_params(2.5),
    )(hidden, *parts, gain[None], bias[None])


def norm_backward_kernel(
    own_ref, core_ref, plane_ref, values_ref, grad_ref, gain_ref, out_ref, low_ref, sums_ref
):
    grad_normed = own_ref[...].astype(F32) + core_ref[...].astype(F32) + plane_ref[...].astype(F32)
    unit, inverse = norm_unit(values_ref[...])
    scaled = grad_normed * gain_ref[...]
    mean_one = jnp.mean(scaled, axis=-1, keepdims=True)
    mean_two = jnp.mean(scaled * unit, axis=-1, keepdims=True)
    grad = grad_ref[...].astype(F32) + inverse * (scaled - mean_one - unit * mean_two)
    out_ref[...] = grad
    low_ref[...] = grad.astype(BF)
    sums_ref[0:1, :] = jnp.sum(grad_normed * unit, axis=0, keepdims=True)
    sums_ref[1:2, :] = jnp.sum(grad_normed, axis=0, keepdims=True)


def norm_backward(parts, values, grad, gain):
    rows, model = values.shape
    return pl.pallas_call(
        norm_backward_kernel,
        out_shape=[
            jax.ShapeDtypeStruct((rows, model), F32),
            jax.ShapeDtypeStruct((rows, model), BF),
            jax.ShapeDtypeStruct((2, model), F32),
        ],
        name="norm_backward",
        **kernel_params(3),
    )(*parts, values, grad, gain[None])


def gelu_and_slope(u):
    cdf = 0.5 * (1.0 + lax.erf(u * ROOT_HALF))
    return (u * cdf).astype(BF), cdf + u * jnp.exp(-0.5 * u * u) * INV_ROOT_TAU


def ffn_forward(x, up_w, down_w):
    u = dot(x, up_w)
    act = gelu_and_slope(u)[0]
    return dot(act, down_w).astype(BF), act, u


def ffn_backward(x, up_w, down_w, u):
    grad = (dot_nt(x, down_w) * gelu_and_slope(u)[1]).astype(BF)
    return dot_nt(grad, up_w).astype(BF), grad


def dot(left, right):
    return jnp.dot(left, right, preferred_element_type=F32)


def gather_start(x):
    plane = flip(x, "zl")
    return x, flip(x, "c"), plane, flip(plane, "c")


def scatter_far(plane, both):
    both = flip(both, "c")
    sent = (plane.astype(F32) + both.astype(F32)).astype(BF)
    return sent, flip(sent, "zl")


def exchange_rest(x):
    return lax.all_to_all(x, "r", 0, 0)


def spread_rest(x, count):
    return exchange_rest(jnp.broadcast_to(x[None], (count,) + x.shape))


def permute_rest(x, count):
    if count != 4:
        return spread_rest(x, count)
    r = lax.axis_index("r")
    pieces = [x] + [lax.ppermute(x, "r", [(i, i ^ k) for i in range(count)]) for k in range(1, count)]
    pieces = jnp.stack(pieces)
    return jnp.stack([lax.dynamic_index_in_dim(pieces, r ^ k, keepdims=False) for k in range(count)])


def weights_kernel(place_ref, up_home_ref, down_home_ref, far_ref, up_ref, down_ref):
    slab, half = up_home_ref.shape[1:]
    up_ref[:, :half] = up_home_ref[0]
    up_ref[:, half:] = far_ref[0, :slab]
    down_ref[0] = down_home_ref[0, 0]
    down_ref[1] = far_ref[0, slab:]


def ffn_weights_here(depth, place, w_up, w_down, far):
    model, hidden_local = w_up.shape[1:]
    half = hidden_local // 2
    count, span = far.shape[:2]
    slab, rows = model // count, half // count
    up, down = pl.pallas_call(
        weights_kernel,
        grid_spec=pltpu.PrefetchScalarGridSpec(
            num_scalar_prefetch=1,
            grid=(count,),
            in_specs=[
                pl.BlockSpec((1, slab, half), lambda j, p: (depth, j, p[0])),
                pl.BlockSpec((1, 1, rows, model), lambda j, p: (depth, p[0], j, 0)),
                pl.BlockSpec((1, span, model), lambda j, p: (j, 0, 0)),
            ],
            out_specs=[
                pl.BlockSpec((slab, hidden_local), lambda j, p: (j, 0)),
                pl.BlockSpec((2, rows, model), lambda j, p: (0, j, 0)),
            ],
        ),
        out_shape=[
            jax.ShapeDtypeStruct((model, hidden_local), BF),
            jax.ShapeDtypeStruct((2, half, model), BF),
        ],
        name="ffn_weights_here",
        **kernel_params(4),
    )(place, w_up, w_down.reshape(LAYERS, 2, half, model), far)
    return up, down.reshape(hidden_local, model)


def ffn_grads_kernel(place_ref, mine_ref, other_ref, *refs):
    up_ref, down_ref = refs[-2:]
    slab, half = up_ref.shape[1], up_ref.shape[2] // 2
    for low in range(2):

        @pl.when(place_ref[0] == low)
        def _(pair=(mine_ref, other_ref) if low == 0 else (other_ref, mine_ref)):
            for n, piece in enumerate(pair):
                up_ref[0, :, n * half : (n + 1) * half] = piece[0, :slab].astype(F32)
                down_ref[0, n] = piece[0, slab:].astype(F32)


def ffn_grads(depth, place, mine, other, hidden_local, stacks=None):
    half = hidden_local // 2
    count, _, model = mine.shape
    slab, rows = model // count, half // count
    span = slab + rows
    shapes = [(LAYERS, model, hidden_local), (LAYERS, 2, half, model)]
    held = [] if stacks is None else list(stacks)
    return pl.pallas_call(
        ffn_grads_kernel,
        grid_spec=pltpu.PrefetchScalarGridSpec(
            num_scalar_prefetch=1,
            grid=(count,),
            in_specs=[pl.BlockSpec((1, span, model), lambda j, p: (j, 0, 0))] * 2
            + [pl.BlockSpec(memory_space=pl.ANY)] * len(held),
            out_specs=[
                pl.BlockSpec((1, slab, hidden_local), lambda j, p: (depth, j, 0)),
                pl.BlockSpec((1, 2, rows, model), lambda j, p: (depth, 0, j, 0)),
            ],
        ),
        out_shape=[jax.ShapeDtypeStruct(shape, F32) for shape in shapes],
        input_output_aliases={3 + n: n for n in range(len(held))},
        name="ffn_grads",
        **kernel_params(4),
    )(place, mine, other, *held)


def dot_nt(left, right, **options):
    return lax.dot_general(
        left, right, (((1,), (1,)), ((), ())), preferred_element_type=F32, **options
    )


def attend_forward_kernel(
    heads,
    own_x_ref,
    core_x_ref,
    plane_x_ref,
    both_x_ref,
    mix_w_ref,
    bias_ref,
    out_w_ref,
    own_ref,
    core_ref,
    plane_ref,
    both_ref,
    x_ref,
    mix_ref,
    o_ref,
    lse_ref,
    q_scr,
    k_scr,
    vt_scr,
    e_scr,
    ot_scr,
):
    blk = bias_ref.shape[1]
    width = heads * HD
    step = pl.program_id(0)

    @pl.when(step == 0)
    def _():
        for n, ref in enumerate((own_x_ref, core_x_ref, plane_x_ref, both_x_ref)):
            rows = slice(n * (blk // 2), (n + 1) * (blk // 2))
            mix = dot_nt(ref[...], mix_w_ref[...]).astype(BF)
            x_ref[rows, :] = ref[...]
            mix_ref[rows, :] = mix
            q_scr[rows, :] = mix[:, :width]
            k_scr[rows, :] = mix[:, width : 2 * width]
            vt_scr[:, rows] = mix[:, 2 * width :].T

    q = q_scr[pl.ds(pl.multiple_of(step * blk, blk), blk), :]
    head_of = lax.broadcasted_iota(jnp.int32, q.shape, 1) // HD
    totals = []
    for h in range(heads):
        q_head = jnp.where(head_of == h, q, jnp.zeros_like(q))
        scores = dot_nt(k_scr[...], q_head) * (LOG2_E / math.sqrt(HD)) + bias_ref[...]
        top = jnp.max(scores, axis=0, keepdims=True)
        expo = jnp.exp2(scores - top)
        total = jnp.sum(expo, axis=0, keepdims=True)
        totals.append(total)
        e_scr[:, h * blk : (h + 1) * blk] = expo.astype(BF)
        lse_ref[h : h + 1, :] = top + jnp.log2(total)
    wide = dot(vt_scr[...], e_scr[...])
    for h in range(heads):
        ot_scr[h * HD : (h + 1) * HD, :] = (
            wide[h * HD : (h + 1) * HD, h * blk : (h + 1) * blk] / totals[h]
        )
    o = ot_scr[...].T
    o_ref[...] = o
    part = dot(o.astype(BF), out_w_ref[...]).astype(BF)

    @pl.when(step == 0)
    def _():
        own_ref[...] = part[: blk // 2]
        core_ref[...] = part[blk // 2 :]

    @pl.when(step == 1)
    def _():
        plane_ref[...] = part[: blk // 2]
        both_ref[...] = part[blk // 2 :]


def attend_forward(blocks, mix_w, bias, out_w):
    part_rows, model = blocks[0].shape
    blk, rows = 2 * part_rows, 4 * part_rows
    width3 = mix_w.shape[0]
    width = out_w.shape[0]
    heads = width // HD
    return pl.pallas_call(
        functools.partial(attend_forward_kernel, heads),
        grid=(2,),
        in_specs=[whole(part_rows, model)] * 4
        + [
            whole(width3, model),
            pl.BlockSpec((rows, blk), lambda i: (0, i)),
            whole(width, model),
        ],
        out_specs=[whole(part_rows, model)] * 4
        + [
            whole(rows, model),
            whole(rows, width3),
            pl.BlockSpec((blk, width), lambda i: (i, 0)),
            pl.BlockSpec((8, blk), lambda i: (0, i)),
        ],
        out_shape=[jax.ShapeDtypeStruct((part_rows, model), BF)] * 4
        + [
            jax.ShapeDtypeStruct((rows, model), BF),
            jax.ShapeDtypeStruct((rows, width3), BF),
            jax.ShapeDtypeStruct((rows, width), F32),
            jax.ShapeDtypeStruct((8, rows), F32),
        ],
        scratch_shapes=[
            pltpu.VMEM((rows, width), BF),
            pltpu.VMEM((rows, width), BF),
            pltpu.VMEM((width, rows), BF),
            pltpu.VMEM((rows, heads * blk), BF),
            pltpu.VMEM((width, blk), F32),
        ],
        name="attend_forward",
        **kernel_params(4),
    )(*blocks, mix_w, bias, out_w)


def attend_backward_kernel(
    heads,
    mix_ref,
    bias_ref,
    mix_w_ref,
    out_w_ref,
    row_refs,
    o_ref,
    lse_ref,
    part_refs,
    grad_ref,
    grad_out_ref,
    q_scr,
    k_scr,
    kt_scr,
    v_scr,
    do_scr,
    p_scr,
    ds_scr,
    qh_scr,
    doh_scr,
    dqt_scr,
    dk_scr,
    dv_scr,
):
    blk = bias_ref.shape[1]
    width = heads * HD
    step = pl.program_id(0)
    scale = 1.0 / math.sqrt(HD)

    @pl.when(step == 0)
    def _():
        q_scr[...] = mix_ref[:, :width]
        k_scr[...] = mix_ref[:, width : 2 * width]
        v_scr[...] = mix_ref[:, 2 * width :]
        kt_scr[...] = k_scr[...].T
        dk_scr[...] = jnp.zeros_like(dk_scr)
        dv_scr[...] = jnp.zeros_like(dv_scr)
        grad_out = jnp.zeros(grad_out_ref.shape, F32)
        for n, ref in enumerate(row_refs):
            rows = slice(n * blk, (n + 1) * blk)
            do_scr[rows, :] = dot_nt(ref[...], out_w_ref[...]).astype(BF)
            grad_out = grad_out + dot(o_ref[rows, :].astype(BF).T, ref[...])
        grad_out_ref[...] = grad_out

    rows = pl.ds(pl.multiple_of(step * blk, blk), blk)
    q = q_scr[rows, :]
    do = do_scr[rows, :]
    head_of = lax.broadcasted_iota(jnp.int32, q.shape, 1) // HD
    pick = (
        lax.broadcasted_iota(jnp.int32, (8, width), 1) // HD
        == lax.broadcasted_iota(jnp.int32, (8, width), 0)
    ).astype(F32)
    inner = dot_nt(pick, do.astype(F32) * o_ref[rows, :], precision=lax.Precision.HIGHEST)
    for h in range(heads):
        cols = slice(h * blk, (h + 1) * blk)
        q_head = jnp.where(head_of == h, q, jnp.zeros_like(q))
        do_head = jnp.where(head_of == h, do, jnp.zeros_like(do))
        qh_scr[cols, :] = q_head
        doh_scr[cols, :] = do_head
        scores = dot_nt(k_scr[...], q_head) * (LOG2_E * scale) + bias_ref[...]
        probs = jnp.exp2(scores - lse_ref[h : h + 1, :])
        p_scr[:, cols] = probs.astype(BF)
        ds = (probs * (dot_nt(v_scr[...], do_head) - inner[h : h + 1, :])).astype(BF)
        ds_scr[:, cols] = ds
        dqt_scr[h * HD : (h + 1) * HD, :] = dot(kt_scr[h * HD : (h + 1) * HD, :], ds) * scale
    dv_scr[...] += dot(p_scr[...], doh_scr[...])
    dk_scr[...] += dot(ds_scr[...], qh_scr[...])
    grad_ref[rows, :width] = dqt_scr[...].T.astype(BF)

    @pl.when(step == pl.num_programs(0) - 1)
    def _():
        grad_ref[:, width : 2 * width] = (dk_scr[...] * scale).astype(BF)
        grad_ref[:, 2 * width :] = dv_scr[...].astype(BF)
        for n, ref in enumerate(part_refs):
            ref[...] = dot(grad_ref[n * blk : (n + 1) * blk, :], mix_w_ref[...]).astype(BF)


def attend_backward(mix, bias, mix_w, out_w, rows_four, o, lse):
    rows, width3 = mix.shape
    blk = rows // 4
    width, model = out_w.shape
    heads = width // HD

    def kernel(*refs):
        attend_backward_kernel(
            heads, *refs[:4], refs[4:8], *refs[8:10], refs[10:14], *refs[14:]
        )

    return pl.pallas_call(
        kernel,
        grid=(4,),
        in_specs=[
            whole(rows, width3),
            pl.BlockSpec((rows, blk), lambda i: (0, i)),
            whole(width3, model),
            whole(width, model),
        ]
        + [whole(blk, model)] * 4
        + [whole(rows, width), pl.BlockSpec((8, blk), lambda i: (0, i))],
        out_specs=[whole(blk, model)] * 4 + [whole(rows, width3), whole(width, model)],
        out_shape=[jax.ShapeDtypeStruct((blk, model), BF)] * 4
        + [
            jax.ShapeDtypeStruct((rows, width3), BF),
            jax.ShapeDtypeStruct((width, model), F32),
        ],
        scratch_shapes=[
            pltpu.VMEM((rows, width), BF),
            pltpu.VMEM((rows, width), BF),
            pltpu.VMEM((width, rows), BF),
            pltpu.VMEM((rows, width), BF),
            pltpu.VMEM((rows, width), BF),
            pltpu.VMEM((rows, heads * blk), BF),
            pltpu.VMEM((rows, heads * blk), BF),
            pltpu.VMEM((heads * blk, width), BF),
            pltpu.VMEM((heads * blk, width), BF),
            pltpu.VMEM((width, blk), F32),
            pltpu.VMEM((rows, width), F32),
            pltpu.VMEM((rows, width), F32),
        ],
        name="attend_backward",
        **kernel_params(6),
    )(mix, bias, mix_w, out_w, *rows_four, o, lse)


def local(
    tokens,
    lengths,
    key_keep,
    ln_gain,
    ln_bias,
    w_qkv,
    w_out,
    w_up,
    w_down,
    readout,
    labels,
    cotangent,
    *,
    rest,
):
    rows_shard, model_width = tokens.shape
    seq_len = key_keep.shape[1]
    local_width = w_qkv.shape[3]
    hidden_local = w_up.shape[2]
    half = hidden_local // 2
    r = lax.axis_index("r")
    c = lax.axis_index("c")
    zh = lax.axis_index("zh")
    zl = lax.axis_index("zl")
    at_home = c == zh
    slab = model_width // rest
    slab_half = half // rest
    slab_attn = 4 * local_width // rest
    span = slab + slab_half

    hidden = rehome(tokens)
    mix_weights = jnp.transpose(w_qkv, (0, 2, 3, 1)).reshape(LAYERS, 3 * local_width, model_width)
    mix_first = rehome(mix_weights[0])
    out_first = rehome(w_out[0])
    place = c.astype(jnp.int32)[None]
    tiled = slab % 16 == 0 and slab_half % 16 == 0

    def far_ffn(depth):
        parts = [
            lax.dynamic_slice(w_up[depth], (r * slab, c * half), (slab, half)),
            lax.dynamic_slice(w_down[depth], (c * half + r * slab_half, 0), (slab_half, model_width)),
        ]
        return jnp.concatenate(parts, axis=0)

    def far_attn(depth):
        both = jnp.concatenate([mix_weights[depth], w_out[depth]], axis=0)
        return lax.dynamic_slice(both, (r * slab_attn, 0), (slab_attn, model_width))

    def ffn_weights(depth, far):
        if tiled:
            return ffn_weights_here(depth, place, w_up, w_down, far)
        up_home = lax.dynamic_slice(w_up[depth], (0, c * half), (model_width, half))
        up_far = far[:, :slab].reshape(model_width, half)
        down_home = lax.dynamic_slice(w_down[depth], (c * half, 0), (half, model_width))
        down_far = far[:, slab:].reshape(half, model_width)
        return (
            jnp.concatenate([up_home, up_far], axis=1),
            jnp.concatenate([down_home, down_far], axis=0),
        )

    def attn_weights(depth, far):
        far = far.reshape(4 * local_width, model_width)
        return (
            jnp.where(at_home, mix_weights[depth], far[: 3 * local_width]),
            jnp.where(at_home, w_out[depth], far[3 * local_width :]),
        )

    col_ids = jnp.arange(seq_len, dtype=jnp.int32)
    allowed = ((col_ids[None, :] < lengths[:, None]) & (key_keep == 1)).astype(jnp.int32)
    allowed = jnp.where(at_home, allowed, flip(allowed, "c")).reshape(2, 2, rows_shard)
    allowed = jnp.where(c == 1, allowed[::-1], allowed)
    allowed = jnp.where(zl == 1, allowed[:, ::-1], allowed)
    allowed = jnp.swapaxes(allowed, 0, 1).reshape(seq_len) == 1
    bias = jnp.where(allowed[:, None] | (col_ids[:, None] == col_ids[None, :]), 0.0, NEG)

    hidden = tie(hidden, bias)
    parts = ()
    saved = []
    for depth in range(LAYERS):
        first, last = depth == 0, depth == LAYERS - 1
        hidden, normed = norm_forward(hidden, parts, ln_gain[depth, 0], ln_bias[depth, 0])
        attn_blocks = gather_start(normed)
        if first:
            mix_w, out_w = mix_first, out_first
        else:
            mix_w, out_w = attn_weights(1, tie(attn_1, normed))
        if first:
            shadow = far_0 = flip(tie(far_ffn(0), normed), "zh")
        else:
            far_1 = flip(tie(far_ffn(1), normed), "zh")
            down_blocks = gather_start(tie(cotangent_home, normed))
            shadow = far_1, down_blocks
        *attn_parts, x, mixed, attended, log_totals = tie(
            attend_forward(attn_blocks, mix_w, bias, out_w), shadow
        )
        sent, came = scatter_far(*attn_parts[2:])
        attn_parts = (attn_parts[0], flip(attn_parts[1], "c"), came)
        if first:
            far_0 = spread_rest(tie(far_0, sent), rest)
            attn_1 = flip(tie(far_attn(1), sent), "zh")
            cotangent_home = rehome(tie(cotangent, attn_parts[2]))
        else:
            far_1 = spread_rest(tie(far_1, sent), rest)
        middle, normed_two = norm_forward(
            hidden, attn_parts, ln_gain[depth, 1], ln_bias[depth, 1]
        )
        ffn_blocks = gather_start(normed_two)
        if first:
            up_w, down_w = ffn_weights(depth, tie(far_0, normed_two))
        else:
            up_w, down_w = ffn_weights(depth, tie(far_1, normed_two))
        ffn_outs, acts, us = zip(*(ffn_forward(b, up_w, down_w) for b in ffn_blocks))
        own, core, plane, both = ffn_outs
        if first:
            plane, both = tie((plane, both), attn_1, cotangent_home)
            attn_1 = spread_rest(attn_1, rest)
            sent, came = scatter_far(plane, both)
            parts = (own, flip(core, "c"), came)
        saved.append(
            dict(
                entry=hidden,
                middle=middle,
                x=x,
                mixed=mixed,
                attended=attended,
                log_totals=log_totals,
                ffn=ffn_blocks,
                act=acts,
                u=us,
                weights=(mix_w, out_w, up_w, down_w),
            )
        )
        hidden = middle
    last_parts = (own, core, plane, both)

    def transposed_dot(left, right):
        left, right = (jnp.concatenate(x, axis=0) for x in (left, right))
        return dot(left.T, right).astype(BF)

    def ffn_blocks_backward(keep, blocks, before=()):
        _, _, up_w, down_w = keep["weights"]
        outs, pres = [None] * 4, [None] * 4
        for k in (3, 2):
            outs[k], pres[k] = ffn_backward(blocks[k], up_w, down_w, keep["u"][k])
        sent, came = scatter_far(*tie(outs[2:], before))
        for k in (1, 0):
            outs[k], pres[k] = ffn_backward(blocks[k], up_w, down_w, keep["u"][k])
        parts = (outs[0], flip(outs[1], "c"), came)
        grad_down = transposed_dot(tie(keep["act"], sent), blocks)
        grad_up = transposed_dot(tie(keep["ffn"], sent), pres)
        return parts, sent, ffn_grad_rows(grad_up, grad_down)

    def ffn_grad_rows(grad_up, grad_down):
        rows = [
            grad_up[:, :half].reshape(rest, slab, half),
            grad_down[:half].reshape(rest, slab_half, model_width),
            grad_up[:, half:].reshape(rest, slab, half),
            grad_down[half:].reshape(rest, slab_half, model_width),
        ]
        return jnp.concatenate(rows, axis=1)

    def finish_ffn(depth, mine, other, stacks):
        if tiled:
            return ffn_grads(depth, place, mine, other, hidden_local, stacks)
        low, high = (jnp.where(c == k, mine, other) for k in (0, 1))
        up = jnp.concatenate([x[:, :slab].reshape(model_width, half) for x in (low, high)], axis=1)
        down = jnp.stack([x[:, slab:span].reshape(half, model_width) for x in (low, high)])
        new = (up.astype(F32), down.astype(F32))
        if stacks is None:
            return [jnp.stack([x] * LAYERS) for x in new]
        return [x.at[depth].set(y) for x, y in zip(stacks, new)]

    def attn_grad_rows(grad_mix, grad_out):
        rows = jnp.concatenate([grad_mix.astype(BF), grad_out.astype(BF)], axis=0)
        return rows.reshape(rest, slab_attn, model_width)

    def finish_attn(mine, other):
        sums = jnp.where(
            at_home, mine[:, span : span + slab_attn], other[:, span : span + slab_attn]
        )
        sums = sums.reshape(4 * local_width, model_width)
        mix = sums[: 3 * local_width].reshape(3, local_width, model_width)
        return mix.astype(F32), sums[3 * local_width :].astype(F32)

    def added(one, two):
        return (one.astype(F32) + two.astype(F32)).astype(BF)

    def attn_backward(keep, row_blocks):
        mix_w, out_w, _, _ = keep["weights"]
        return attend_backward(
            keep["mixed"], bias, mix_w, out_w, row_blocks, keep["attended"], keep["log_totals"]
        )

    def sum_first(x):
        return jnp.sum(x.astype(F32), axis=0)

    keep = saved[1]
    parts, sent, ffn_a = ffn_blocks_backward(keep, down_blocks)
    ffn_a = exchange_rest(ffn_a)
    grad, low, sums_11 = norm_backward(parts, keep["middle"], cotangent_home, ln_gain[1, 1])
    row_blocks = gather_start(low)

    own, core, plane, both = tie(last_parts, row_blocks)
    _, plane = scatter_far(plane, both)
    core = flip(core, "c")
    *parts, mix_grad, grad_out = tie(attn_backward(keep, row_blocks), plane, core, ffn_a)
    sent, came = scatter_far(*parts[2:])
    parts = (parts[0], flip(parts[1], "c"), came)
    ffn_a = sum_first(tie(ffn_a, sent)).astype(BF)
    grad_mix = dot(tie(mix_grad, sent).T, keep["x"])
    attn_a = attn_grad_rows(grad_mix, grad_out)
    grad, low, sums_10 = norm_backward(parts, keep["entry"], grad, ln_gain[1, 0])
    attn_a = exchange_rest(attn_a)

    down_blocks = gather_start(low)
    keep = saved[0]
    parts, sent, ffn_b = ffn_blocks_backward(keep, down_blocks)
    attn_a = sum_first(tie(attn_a, sent)).astype(BF)
    parts, ffn_b = tie((parts, ffn_b), attn_a)
    ffn_b = exchange_rest(ffn_b)
    grad, low, sums_01 = norm_backward(parts, keep["middle"], grad, ln_gain[0, 1])
    row_blocks = gather_start(low)
    plane, core = tie((plane, core), low)
    final = saved[1]["middle"] + own.astype(F32) + core.astype(F32) + plane.astype(F32)
    held = jnp.concatenate([ffn_a[span:], attn_a], axis=0)
    came_a = flip(tie(held, low), "zh")

    *parts, mix_grad, grad_out = tie(attn_backward(keep, row_blocks), ffn_b, came_a)
    sent, came = scatter_far(*parts[2:])
    parts = (parts[0], flip(parts[1], "c"), came)
    ffn_b = sum_first(tie(ffn_b, sent))
    came_b = flip(ffn_b[span:].astype(BF), "zh")
    grad_mix = dot(tie(mix_grad, sent).T, keep["x"])
    attn_b = exchange_rest(attn_grad_rows(grad_mix, grad_out))
    grad, low, sums_00 = norm_backward(parts, keep["entry"], grad, ln_gain[0, 0])

    first_of_four = (zh == 0) & (zl == 0)
    count = jnp.where(first_of_four, lengths[0], 0).astype(F32)
    sums = jnp.stack([sums_00, sums_01, sums_10, sums_11])
    small = jnp.concatenate(
        [
            sums[:, 0],
            sums[:, 1],
            jnp.broadcast_to(count, (1, model_width)),
            jnp.zeros((16 - 4 * LAYERS - 1, model_width), F32),
        ],
        axis=0,
    )
    small = small + flip(small, "zl")

    def in_two(x):
        high = lax.reduce_precision(x, 8, 7)
        return jnp.concatenate([high, x - high], axis=0).astype(BF)

    def from_two(x):
        high, rest_of_it = jnp.split(x.astype(F32), 2, axis=-2)
        return high + rest_of_it

    attn_b = sum_first(tie(attn_b, low)).astype(BF)
    sent_c = jnp.concatenate([attn_b, in_two(small)], axis=0)
    came_c = flip(sent_c, "zh")
    small = small + from_two(came_c[slab_attn:])
    rows_b = jnp.concatenate(
        [
            (ffn_b[:span] + came_b.astype(F32)).astype(BF),
            added(attn_b, came_c[:slab_attn]),
            in_two(small),
        ],
        axis=0,
    )
    rows_b = spread_rest(rows_b, rest)
    layer_out = rehome(tie(final.astype(BF), low))
    grad_tokens = rehome(low)
    row_ids = (2 * zh + zl) * rows_shard + jnp.arange(rows_shard, dtype=jnp.int32)
    live_rows = row_ids < lengths[0]
    logits = dot(layer_out, readout)
    top = jnp.max(logits, axis=-1, keepdims=True)
    log_total = top[:, 0] + jnp.log(jnp.sum(jnp.exp(logits - top), axis=-1))
    classes = jnp.arange(logits.shape[1], dtype=jnp.int32)
    picked = jnp.sum(jnp.where(labels[:, None] == classes[None, :], logits, 0.0), axis=-1)
    label_logprob = jnp.where(live_rows, picked - log_total, jnp.zeros_like(log_total))

    rows_a = added(jnp.concatenate([ffn_a[:span], attn_a], axis=0), came_a)
    rows_a = spread_rest(tie(rows_a, rows_b), rest)
    rows_b, layer_out, label_logprob, grad_tokens = tie(
        (rows_b, layer_out, label_logprob, grad_tokens)
    )
    rows_b = (rows_b, flip(rows_b, "c"))
    ffn_stacks = finish_ffn(0, *rows_b, None)
    attn_b = finish_attn(*rows_b)
    small = sum(jnp.sum(from_two(x[:, span + slab_attn :]), axis=0) for x in rows_b)
    rows_a, ffn_stacks, attn_b, small = tie((rows_a, ffn_stacks, attn_b, small))
    rows_a = (rows_a, flip(rows_a, "c"))
    grads_up, grads_down = finish_ffn(1, *rows_a, ffn_stacks)
    attn_a = finish_attn(*rows_a)
    grads_mix, grads_out = (jnp.stack(pair) for pair in zip(attn_b, attn_a))
    grads_mix = jnp.transpose(grads_mix, (0, 3, 1, 2))
    grad_tokens = grad_tokens.astype(F32)
    gain_total = small[: 2 * LAYERS].reshape(LAYERS, 2, model_width)
    shift_total = small[2 * LAYERS : 4 * LAYERS].reshape(LAYERS, 2, model_width)
    token_count = small[4 * LAYERS, 0].astype(jnp.int32)
    return (
        layer_out,
        grad_tokens,
        gain_total,
        shift_total,
        grads_mix,
        grads_out,
        grads_up,
        grads_down.reshape(LAYERS, hidden_local, model_width),
        label_logprob,
        token_count,
    )


def solution(mesh):
    batch, model = mesh.devices.shape
    rest = batch // 2
    fine = Mesh(mesh.devices.reshape(rest, 2, 2, model // 2), ("r", "c", "zh", "zl"))
    dp = ("r", "c")
    mp = ("zh", "zl")
    both = dp + mp
    in_specs = (
        P(both, None),
        P(dp),
        P(dp, None),
        P(),
        P(),
        P(None, None, None, mp),
        P(None, mp, None),
        P(None, None, mp),
        P(None, mp, None),
        P(),
        P(both),
        P(both, None),
    )
    out_specs = (
        P(both, None),
        P(both, None),
        P(),
        P(),
        P(None, None, None, mp),
        P(None, mp, None),
        P(None, None, mp),
        P(None, mp, None),
        P(both),
        P(),
    )

    def body(*args):
        return local(*args, rest=rest)

    return jax.shard_map(body, mesh=fine, in_specs=in_specs, out_specs=out_specs, check_vma=False)
```

profile of v0, /device:TPU:0, one launch (start us, length us, event | category | flops | bytes accessed | tf_op | source)
XLA Modules:
  0.0 509.4 jit_solution(10012923702144643463)
XLA Ops:
  6.4 6.4 %collective-permute-start.5 = (bf16[480,640]{1,0:T(8,128)(2,1)}, bf16[480,640]{1,0:T(8,128)(2,1)}, u32[]{:S(2)}, u32[]{:S(2)}) collective-permute-start(bf16[480,640]{1,0:T(8,128)(2,1)} %bitcast.5), channel_id=1, source_target_pairs={{0,0},{1,1},{2,4},{3,5},{4,2},{5,3},{6,6},{7,7},{8,8},{9,9},{10,12... | collective-permute-start | bytes 1843208 | tf_op jit(solution)/shard_map/ppermute | solution.py:35
  24.2 6.0 %collective-permute-start.2 = (bf16[256,640]{1,0:T(8,128)(2,1)}, bf16[256,640]{1,0:T(8,128)(2,1)}, u32[]{:S(2)}, u32[]{:S(2)}) collective-permute-start(bf16[256,640]{1,0:T(8,128)(2,1)} %get-tuple-element.157.own_x_ref), channel_id=1, source_target_pairs={{0,4},{4,0},{1,5},{5,1},{2,6},{6,2},{3,7},{7,3},{8,12},{12,8},{9,1... | collective-permute-start | bytes 983048 | tf_op jit(solution)/shard_map/ppermute | solution.py:39
  30.2 7.3 %collective-permute-done.3.plane_x_ref = bf16[256,640]{1,0:T(8,128)(2,1)} collective-permute-done((bf16[256,640]{1,0:T(8,128)(2,1)}, bf16[256,640]{1,0:T(8,128)(2,1)}, u32[]{:S(2)}, u32[]{:S(2)}) %collective-permute-start.3) | collective-permute-done | bytes 327712 | tf_op jit(solution)/shard_map/ppermute | solution.py:39
  45.9 14.0 %attend_forward.2 = (bf16[256,640]{1,0:T(8,128)(2,1)}, bf16[256,640]{1,0:T(8,128)(2,1)}, bf16[256,640]{1,0:T(8,128)(2,1)}, bf16[256,640]{1,0:T(8,128)(2,1)}, bf1...) custom-call(bf16[256,640]{1,0:T(8,128)(2,1)} %get-tuple-element.157.own_x_ref, ...), custom_call_target="tpu_custom_call" | custom-call | flops 4600000000 | bytes 1048576 | tf_op jit(solution)/shard_map/attend_forward/pallas_call | solution.py:326
  59.9 4.9 collective-permute-done.7
  75.4 8.3 %collective-permute-done.10.refs_2_ = bf16[256,640]{1,0:T(8,128)(2,1)S(1)} collective-permute-done((bf16[256,640]{1,0:T(8,128)(2,1)S(1)}, bf16[256,640]{1,0:T(8,128)(2,1)S(1)}, u32[]{:S(2)}, u32[]{:S(2)}) %collective-permute-start.10) | collective-permute-done | bytes 327712 | tf_op jit(solution)/shard_map/ppermute | solution.py:39
  95.1 6.7 %collective-permute-done.13 = bf16[256,640]{1,0:T(8,128)(2,1)} collective-permute-done((bf16[256,640]{1,0:T(8,128)(2,1)}, bf16[256,640]{1,0:T(8,128)(2,1)}, u32[]{:S(2)}, u32[]{:S(2)}) %collective-permute-start.13) | collective-permute-done | bytes 327712 | tf_op jit(solution)/shard_map/ppermute | solution.py:39
  103.2 4.5 all-to-all-start.1
  107.7 4.4 ffn_weights_here.2
  130.2 4.7 collective-permute-done.18.refs_2_
  142.2 7.0 %collective-permute-done.20.plane_x_ref = bf16[256,640]{1,0:T(8,128)(2,1)} collective-permute-done((bf16[256,640]{1,0:T(8,128)(2,1)}, bf16[256,640]{1,0:T(8,128)(2,1)}, u32[]{:S(2)}, u32[]{:S(2)}) %collective-permute-start.20) | collective-permute-done | bytes 327712 | tf_op jit(solution)/shard_map/ppermute | solution.py:39
  155.9 14.0 %attend_forward.3 = (bf16[256,640]{1,0:T(8,128)(2,1)}, bf16[256,640]{1,0:T(8,128)(2,1)}, bf16[256,640]{1,0:T(8,128)(2,1)}, bf16[256,640]{1,0:T(8,128)(2,1)}, bf1...) custom-call(bf16[256,640]{1,0:T(8,128)(2,1)} %get-tuple-element.181.own_x_ref, ...), custom_call_target="tpu_custom_call" | custom-call | flops 4600000000 | bytes 1048576 | tf_op jit(solution)/shard_map/attend_forward/pallas_call | solution.py:326
  177.5 4.6 all-to-all-start.2
  184.0 8.5 %collective-permute-done.28.refs_2_ = bf16[256,640]{1,0:T(8,128)(2,1)S(1)} collective-permute-done((bf16[256,640]{1,0:T(8,128)(2,1)}, bf16[256,640]{1,0:T(8,128)(2,1)S(1)}, u32[]{:S(2)}, u32[]{:S(2)}) %collective-permute-start.28) | collective-permute-done | bytes 327712 | tf_op jit(solution)/shard_map/ppermute | solution.py:39
  196.4 8.9 %collective-permute-done.31 = bf16[256,640]{1,0:T(8,128)(2,1)} collective-permute-done((bf16[256,640]{1,0:T(8,128)(2,1)}, bf16[256,640]{1,0:T(8,128)(2,1)}, u32[]{:S(2)}, u32[]{:S(2)}) %collective-permute-start.31) | collective-permute-done | bytes 327712 | tf_op jit(solution)/shard_map/ppermute | solution.py:39
  206.5 4.4 ffn_weights_here.3
  237.3 4.9 all-to-all-start.3
  248.3 7.1 %collective-permute-done.36.refs_6_ = bf16[256,640]{1,0:T(8,128)(2,1)S(1)} collective-permute-done((bf16[256,640]{1,0:T(8,128)(2,1)}, bf16[256,640]{1,0:T(8,128)(2,1)S(1)}, u32[]{:S(2)}, u32[]{:S(2)}) %collective-permute-start.36) | collective-permute-done | bytes 327712 | tf_op jit(solution)/shard_map/ppermute | solution.py:39
  260.8 22.9 %attend_backward.2 = (bf16[256,640]{1,0:T(8,128)(2,1)}, bf16[256,640]{1,0:T(8,128)(2,1)}, bf16[256,640]{1,0:T(8,128)(2,1)}, bf16[256,640]{1,0:T(8,128)(2,1)}, bf...) custom-call(bf16[1024,480]{1,0:T(8,128)(2,1)} %get-tuple-element.193.refs_0_, f32[1024,1024]{1,0:T(8,128)} %fusion.1.bias_ref.refs_1_, ...), custom_call_target="tpu_custom_call" | custom-call | flops 6899999744 | bytes 1048576 | tf_op jit(solution)/shard_map/attend_backward/pallas_call | solution.py:450
  290.8 4.4 all-to-all-start.4
  304.5 5.2 %collective-permute-done.46 = bf16[256,640]{1,0:T(8,128)(2,1)S(1)} collective-permute-done((bf16[256,640]{1,0:T(8,128)(2,1)}, bf16[256,640]{1,0:T(8,128)(2,1)S(1)}, u32[]{:S(2)}, u32[]{:S(2)}) %collective-permute-start.46) | collective-permute-done | bytes 327712 | tf_op jit(solution)/shard_map/ppermute | solution.py:39
  327.6 4.5 all-to-all-start.5
  339.7 4.5 collective-permute-done.51.refs_6_
  351.2 22.9 %attend_backward.3 = (bf16[256,640]{1,0:T(8,128)(2,1)}, bf16[256,640]{1,0:T(8,128)(2,1)}, bf16[256,640]{1,0:T(8,128)(2,1)}, bf16[256,640]{1,0:T(8,128)(2,1)}, bf...) custom-call(bf16[1024,480]{1,0:T(8,128)(2,1)} %get-tuple-element.249.refs_0_, f32[1024,1024]{1,0:T(8,128)} %fusion.1.bias_ref.refs_1_, ...), custom_call_target="tpu_custom_call" | custom-call | flops 6899999744 | bytes 1048576 | tf_op jit(solution)/shard_map/attend_backward/pallas_call | solution.py:450
  391.2 6.7 %collective-permute-done.57.plane_ref = bf16[256,640]{1,0:T(8,128)(2,1)} collective-permute-done((bf16[256,640]{1,0:T(8,128)(2,1)}, bf16[256,640]{1,0:T(8,128)(2,1)}, u32[]{:S(2)}, u32[]{:S(2)}) %collective-permute-start.57) | collective-permute-done | bytes 327712 | tf_op jit(solution)/shard_map/ppermute | solution.py:39
  402.0 4.0 collective-permute-done.58
  408.0 10.8 %collective-permute-done.59 = bf16[192,640]{1,0:T(8,128)(2,1)S(1)} collective-permute-done((bf16[192,640]{1,0:T(8,128)(2,1)S(1)}, bf16[192,640]{1,0:T(8,128)(2,1)S(1)}, u32[]{:S(2)}, u32[]{:S(2)}) %collective-permute-start.59) | collective-permute-done | bytes 245792 | tf_op jit(solution)/shard_map/ppermute | solution.py:39
  420.7 4.7 all-to-all-start.7
  429.0 27.4 %all-to-all-done.7.mine_ref = bf16[4,512,640]{2,1,0:T(8,128)(2,1)} async-done(((bf16[4,512,640]{2,1,0:T(8,128)(2,1)}), bf16[4,512,640]{2,1,0:T(8,128)(2,1)}, u32[]{:S(2)}, u32[]{:S(2)}) %all-to-all-start.7) | async-done | bytes 2621472 | tf_op jit(solution)/shard_map/all_to_all | solution.py:152
  467.6 5.1 %ffn_grads.2 = (f32[2,640,1280]{2,1,0:T(8,128)}, f32[2,2,640,640]{3,2,1,0:T(8,128)}) custom-call(s32[1]{0:T(128)} %bitcast.11.place_ref, bf16[4,512,640]{2,1,0:T(8,128)(2,1)} %all-to-all-done.7.mine_ref, bf16[4,512,640]{2,1,0:T(8,128)(2,1)} %collective-permute-done.62.other_ref), custom_call_target="tpu_custom_call" | custom-call | flops 4600000000 | bytes 1048576 | tf_op jit(solution)/shard_map/ffn_grads/pallas_call | solution.py:225
  472.8 19.8 %all-to-all-done.8.mine_ref = bf16[4,480,640]{2,1,0:T(8,128)(2,1)S(1)} async-done(((bf16[4,480,640]{2,1,0:T(8,128)(2,1)}), bf16[4,480,640]{2,1,0:T(8,128)(2,1)S(1)}, u32[]{:S(2)}, u32[]{:S(2)}) %all-to-all-start.8) | async-done | bytes 2457632 | tf_op jit(solution)/shard_map/all_to_all | solution.py:152
  501.9 5.1 %ffn_grads.3 = (f32[2,640,1280]{2,1,0:T(8,128)}, f32[2,2,640,640]{3,2,1,0:T(8,128)}) custom-call(s32[1]{0:T(128)} %bitcast.11.place_ref, bf16[4,480,640]{2,1,0:T(8,128)(2,1)} %copy-done.3, bf16[4,480,640]{2,1,0:T(8,128)(2,1)} %collective-permute-done.63.other_ref, ...), custom_call_target="tpu_custom_call", output_to_operand_aliasing={{0}: (3, {}), {1}: (4, {})} | custom-call | flops 4600000000 | bytes 1048576 | tf_op jit(solution)/shard_map/ffn_grads/pallas_call | solution.py:225
  (413 shorter events, 230.0 us)
Async XLA Ops:
  2.5 14.8 %collective-permute-start = (bf16[256,640]{1,0:T(8,128)(2,1)}, bf16[256,640]{1,0:T(8,128)(2,1)S(1)}, u32[]{:S(2)}, u32[]{:S(2)}) collective-permute-start(bf16[256,640]{1,0:T(8,128)(2,1)} %param.12), channel_id=1, source_target_pairs={{0,0},{1,1},{2,4},{3,5},{4,2},{5,3},{6,6},{7,7},{8,8},{9,9},{10,12... | collective-permute-start | bytes 983048 | tf_op jit(solution)/shard_map/ppermute | solution.py:35
  6.4 39.5 %collective-permute-start.5 = (bf16[480,640]{1,0:T(8,128)(2,1)}, bf16[480,640]{1,0:T(8,128)(2,1)}, u32[]{:S(2)}, u32[]{:S(2)}) collective-permute-start(bf16[480,640]{1,0:T(8,128)(2,1)} %bitcast.5), channel_id=1, source_target_pairs={{0,0},{1,1},{2,4},{3,5},{4,2},{5,3},{6,6},{7,7},{8,8},{9,9},{10,12... | collective-permute-start | bytes 1843208 | tf_op jit(solution)/shard_map/ppermute | solution.py:35
  12.8 33.1 %collective-permute-start.6 = (bf16[160,640]{1,0:T(8,128)(2,1)S(1)}, bf16[160,640]{1,0:T(8,128)(2,1)}, u32[]{:S(2)}, u32[]{:S(2)}) collective-permute-start(bf16[160,640]{1,0:T(8,128)(2,1)S(1)} %get-tuple-element.319), channel_id=1, source_target_pairs={{0,0},{1,1},{2,4},{3,5},{4,2},{5,3},{6,6},{7,7},{8,8},{9,9},{10,12... | collective-permute-start | bytes 614408 | tf_op jit(solution)/shard_map/ppermute | solution.py:35
  20.2 17.3 %collective-permute-start.3 = (bf16[256,640]{1,0:T(8,128)(2,1)}, bf16[256,640]{1,0:T(8,128)(2,1)}, u32[]{:S(2)}, u32[]{:S(2)}) collective-permute-start(bf16[256,640]{1,0:T(8,128)(2,1)} %get-tuple-element.157.own_x_ref), channel_id=1, source_target_pairs={{0,1},{1,0},{2,3},{3,2},{4,5},{5,4},{6,7},{7,6},{8,9},{9,8},{10,11... | collective-permute-start | bytes 983048 | tf_op jit(solution)/shard_map/ppermute | solution.py:39
  24.2 21.7 %collective-permute-start.2 = (bf16[256,640]{1,0:T(8,128)(2,1)}, bf16[256,640]{1,0:T(8,128)(2,1)}, u32[]{:S(2)}, u32[]{:S(2)}) collective-permute-start(bf16[256,640]{1,0:T(8,128)(2,1)} %get-tuple-element.157.own_x_ref), channel_id=1, source_target_pairs={{0,4},{4,0},{1,5},{5,1},{2,6},{6,2},{3,7},{7,3},{8,12},{12,8},{9,1... | collective-permute-start | bytes 983048 | tf_op jit(solution)/shard_map/ppermute | solution.py:39
  42.4 22.4 %collective-permute-start.7 = (bf16[320,640]{1,0:T(8,128)(2,1)S(1)}, bf16[320,640]{1,0:T(8,128)(2,1)S(1)}, u32[]{:S(2)}, u32[]{:S(2)}) collective-permute-start(bf16[320,640]{1,0:T(8,128)(2,1)S(1)} %pad_maximum_fusion.8), channel_id=1, source_target_pairs={{0,2},{2,0},{1,3},{3,1},{4,6},{6,4},{5,7},{7,5},{8,10},{10,8},{9,1... | collective-permute-start | bytes 1228808 | tf_op jit(solution)/shard_map/ppermute | solution.py:39
  69.7 32.1 %all-to-all-start = ((bf16[4,320,640]{2,1,0:T(8,128)(2,1)}), bf16[4,320,640]{2,1,0:T(8,128)(2,1)S(1)}, u32[]{:S(2)}, u32[]{:S(2)}) async-start(bf16[4,320,640]{2,1,0:T(8,128)(2,1)} %broadcast_in_dim.32), calls=%async_computation | async-start | bytes 3276800 | tf_op jit(solution)/shard_map/all_to_all | solution.py:152
  86.9 14.9 %collective-permute-start.13 = (bf16[256,640]{1,0:T(8,128)(2,1)}, bf16[256,640]{1,0:T(8,128)(2,1)}, u32[]{:S(2)}, u32[]{:S(2)}) collective-permute-start(bf16[256,640]{1,0:T(8,128)(2,1)} %get-tuple-element.235), channel_id=1, source_target_pairs={{0,1},{1,0},{2,3},{3,2},{4,5},{5,4},{6,7},{7,6},{8,9},{9,8},{10,11... | collective-permute-start | bytes 983048 | tf_op jit(solution)/shard_map/ppermute | solution.py:39
  87.8 13.9 %collective-permute-start.15 = (bf16[160,640]{1,0:T(8,128)(2,1)S(1)}, bf16[160,640]{1,0:T(8,128)(2,1)S(1)}, u32[]{:S(2)}, u32[]{:S(2)}) collective-permute-start(bf16[160,640]{1,0:T(8,128)(2,1)S(1)} %fusion.100), channel_id=1, source_target_pairs={{0,2},{2,0},{1,3},{3,1},{4,6},{6,4},{5,7},{7,5},{8,10},{10,8},{9,1... | collective-permute-start | bytes 614408 | tf_op jit(solution)/shard_map/ppermute | solution.py:39
  91.3 29.2 %collective-permute-start.11 = (bf16[256,640]{1,0:T(8,128)(2,1)}, bf16[256,640]{1,0:T(8,128)(2,1)}, u32[]{:S(2)}, u32[]{:S(2)}) collective-permute-start(bf16[256,640]{1,0:T(8,128)(2,1)} %get-tuple-element.235), channel_id=1, source_target_pairs={{0,4},{4,0},{1,5},{5,1},{2,6},{6,2},{3,7},{7,3},{8,12},{12,8},{9,1... | collective-permute-start | bytes 983048 | tf_op jit(solution)/shard_map/ppermute | solution.py:39
  91.3 28.9 %collective-permute-start.16 = (bf16[256,640]{1,0:T(8,128)(2,1)}, bf16[256,640]{1,0:T(8,128)(2,1)}, u32[]{:S(2)}, u32[]{:S(2)}) collective-permute-start(bf16[256,640]{1,0:T(8,128)(2,1)} %param.23), channel_id=1, source_target_pairs={{0,0},{1,1},{2,4},{3,5},{4,2},{5,3},{6,6},{7,7},{8,8},{9,9},{10,12... | collective-permute-start | bytes 983048 | tf_op jit(solution)/shard_map/ppermute | solution.py:35
  101.8 13.8 %collective-permute-start.14 = (bf16[256,640]{1,0:T(8,128)(2,1)}, bf16[256,640]{1,0:T(8,128)(2,1)}, u32[]{:S(2)}, u32[]{:S(2)}) collective-permute-start(bf16[256,640]{1,0:T(8,128)(2,1)} %collective-permute-done.13), channel_id=1, source_target_pairs={{0,4},{4,0},{1,5},{5,1},{2,6},{6,2},{3,7},{7,3},{8,12},{12,8},{9,1... | collective-permute-start | bytes 983048 | tf_op jit(solution)/shard_map/ppermute | solution.py:39
  103.2 38.6 %all-to-all-start.1 = ((bf16[4,160,640]{2,1,0:T(8,128)(2,1)}), bf16[4,160,640]{2,1,0:T(8,128)(2,1)S(1)}, u32[]{:S(2)}, u32[]{:S(2)}) async-start(bf16[4,160,640]{2,1,0:T(8,128)(2,1)} %broadcast_in_dim.34), calls=%async_computation.1 | async-start | bytes 1638400 | tf_op jit(solution)/shard_map/all_to_all | solution.py:152
  150.0 20.0 %collective-permute-start.23 = (bf16[256,640]{1,0:T(8,128)(2,1)}, bf16[256,640]{1,0:T(8,128)(2,1)S(1)}, u32[]{:S(2)}, u32[]{:S(2)}) collective-permute-start(bf16[256,640]{1,0:T(8,128)(2,1)} %collective-permute-done.16.grad_ref), channel_id=1, source_target_pairs={{0,4},{4,0},{1,5},{5,1},{2,6},{6,2},{3,7},{7,3},{8,12},{12,8},{9,1... | collective-permute-start | bytes 983048 | tf_op jit(solution)/shard_map/ppermute | solution.py:39
  150.5 22.0 %collective-permute-start.22 = (bf16[320,640]{1,0:T(8,128)(2,1)S(1)}, bf16[320,640]{1,0:T(8,128)(2,1)S(1)}, u32[]{:S(2)}, u32[]{:S(2)}) collective-permute-start(bf16[320,640]{1,0:T(8,128)(2,1)S(1)} %copy-done.30), channel_id=1, source_target_pairs={{0,2},{2,0},{1,3},{3,1},{4,6},{6,4},{5,7},{7,5},{8,10},{10,8},{9,1... | collective-permute-start | bytes 1228808 | tf_op jit(solution)/shard_map/ppermute | solution.py:39
  155.1 17.5 %collective-permute-start.25 = (bf16[256,640]{1,0:T(8,128)(2,1)S(1)}, bf16[256,640]{1,0:T(8,128)(2,1)S(1)}, u32[]{:S(2)}, u32[]{:S(2)}) collective-permute-start(bf16[256,640]{1,0:T(8,128)(2,1)S(1)} %collective-permute-done.24), channel_id=1, source_target_pairs={{0,4},{4,0},{1,5},{5,1},{2,6},{6,2},{3,7},{7,3},{8,12},{12,8},{9,1... | collective-permute-start | bytes 983048 | tf_op jit(solution)/shard_map/ppermute | solution.py:39
  177.5 27.8 %all-to-all-start.2 = ((bf16[4,320,640]{2,1,0:T(8,128)(2,1)}), bf16[4,320,640]{2,1,0:T(8,128)(2,1)S(1)}, u32[]{:S(2)}, u32[]{:S(2)}) async-start(bf16[4,320,640]{2,1,0:T(8,128)(2,1)} %broadcast_in_dim.35), calls=%async_computation.2 | async-start | bytes 3276800 | tf_op jit(solution)/shard_map/all_to_all | solution.py:152
  196.4 25.9 %collective-permute-start.29 = (bf16[256,640]{1,0:T(8,128)(2,1)}, bf16[256,640]{1,0:T(8,128)(2,1)}, u32[]{:S(2)}, u32[]{:S(2)}) collective-permute-start(bf16[256,640]{1,0:T(8,128)(2,1)} %get-tuple-element.219), channel_id=1, source_target_pairs={{0,4},{4,0},{1,5},{5,1},{2,6},{6,2},{3,7},{7,3},{8,12},{12,8},{9,1... | collective-permute-start | bytes 983048 | tf_op jit(solution)/shard_map/ppermute | solution.py:39
  226.3 15.8 %collective-permute-start.30 = (bf16[256,640]{1,0:T(8,128)(2,1)}, bf16[256,640]{1,0:T(8,128)(2,1)}, u32[]{:S(2)}, u32[]{:S(2)}) collective-permute-start(bf16[256,640]{1,0:T(8,128)(2,1)} %convolution_convert_fusion.16), channel_id=1, source_target_pairs={{0,4},{4,0},{1,5},{5,1},{2,6},{6,2},{3,7},{7,3},{8,12},{12,8},{9,1... | collective-permute-start | bytes 983048 | tf_op jit(solution)/shard_map/ppermute | solution.py:39
  227.9 14.3 %collective-permute-start.34 = (bf16[256,640]{1,0:T(8,128)(2,1)S(1)}, bf16[256,640]{1,0:T(8,128)(2,1)}, u32[]{:S(2)}, u32[]{:S(2)}) collective-permute-start(bf16[256,640]{1,0:T(8,128)(2,1)S(1)} %add_convert_fusion.6), channel_id=1, source_target_pairs={{0,1},{1,0},{2,3},{3,2},{4,5},{5,4},{6,7},{7,6},{8,9},{9,8},{10,11... | collective-permute-start | bytes 983048 | tf_op jit(solution)/shard_map/ppermute | solution.py:39
  237.3 46.5 %all-to-all-start.3 = ((bf16[4,640,640]{2,1,0:T(8,128)(2,1)}), bf16[4,640,640]{2,1,0:T(8,128)(2,1)}, u32[]{:S(2)}, u32[]{:S(2)}) async-start(bf16[4,640,640]{2,1,0:T(8,128)(2,1)} %pad_maximum_fusion), calls=%async_computation.3 | async-start | bytes 6553600 | tf_op jit(solution)/shard_map/all_to_all | solution.py:152
  258.1 25.7 %collective-permute-start.40 = (bf16[256,640]{1,0:T(8,128)(2,1)S(1)}, bf16[256,640]{1,0:T(8,128)(2,1)}, u32[]{:S(2)}, u32[]{:S(2)}) collective-permute-start(bf16[256,640]{1,0:T(8,128)(2,1)S(1)} %convolution_convert_fusion.12), channel_id=1, source_target_pairs={{0,4},{4,0},{1,5},{5,1},{2,6},{6,2},{3,7},{7,3},{8,12},{12,8},{9,1... | collective-permute-start | bytes 983048 | tf_op jit(solution)/shard_map/ppermute | solution.py:39
  259.4 24.3 %collective-permute-start.39 = (bf16[256,640]{1,0:T(8,128)(2,1)S(1)}, bf16[256,640]{1,0:T(8,128)(2,1)}, u32[]{:S(2)}, u32[]{:S(2)}) collective-permute-start(bf16[256,640]{1,0:T(8,128)(2,1)S(1)} %add_convert_fusion.5), channel_id=1, source_target_pairs={{0,1},{1,0},{2,3},{3,2},{4,5},{5,4},{6,7},{7,6},{8,9},{9,8},{10,11... | collective-permute-start | bytes 983048 | tf_op jit(solution)/shard_map/ppermute | solution.py:39
  290.8 33.3 %all-to-all-start.4 = ((bf16[4,160,640]{2,1,0:T(8,128)(2,1)}), bf16[4,160,640]{2,1,0:T(8,128)(2,1)}, u32[]{:S(2)}, u32[]{:S(2)}) async-start(bf16[4,160,640]{2,1,0:T(8,128)(2,1)} %bitcast.33), calls=%async_computation.4 | async-start | bytes 1638400 | tf_op jit(solution)/shard_map/all_to_all | solution.py:152
  327.6 49.9 %all-to-all-start.5 = ((bf16[4,640,640]{2,1,0:T(8,128)(2,1)}), bf16[4,640,640]{2,1,0:T(8,128)(2,1)S(1)}, u32[]{:S(2)}, u32[]{:S(2)}) async-start(bf16[4,640,640]{2,1,0:T(8,128)(2,1)} %pad_maximum_fusion.1), calls=%async_computation.5 | async-start | bytes 6553600 | tf_op jit(solution)/shard_map/all_to_all | solution.py:152
  346.3 31.2 %collective-permute-start.53 = (bf16[480,640]{1,0:T(8,128)(2,1)S(1)}, bf16[480,640]{1,0:T(8,128)(2,1)}, u32[]{:S(2)}, u32[]{:S(2)}) collective-permute-start(bf16[480,640]{1,0:T(8,128)(2,1)S(1)} %pad_maximum_fusion.6), channel_id=1, source_target_pairs={{0,2},{2,0},{1,3},{3,1},{4,6},{6,4},{5,7},{7,5},{8,10},{10,8},{9,1... | collective-permute-start | bytes 1843208 | tf_op jit(solution)/shard_map/ppermute | solution.py:39
  377.7 13.5 %collective-permute-start.56 = (bf16[256,640]{1,0:T(8,128)(2,1)}, bf16[256,640]{1,0:T(8,128)(2,1)}, u32[]{:S(2)}, u32[]{:S(2)}) collective-permute-start(bf16[256,640]{1,0:T(8,128)(2,1)} %get-tuple-element.273), channel_id=1, source_target_pairs={{0,4},{4,0},{1,5},{5,1},{2,6},{6,2},{3,7},{7,3},{8,12},{12,8},{9,1... | collective-permute-start | bytes 983048 | tf_op jit(solution)/shard_map/ppermute | solution.py:39
  381.4 16.5 %collective-permute-start.57 = (bf16[256,640]{1,0:T(8,128)(2,1)}, bf16[256,640]{1,0:T(8,128)(2,1)}, u32[]{:S(2)}, u32[]{:S(2)}) collective-permute-start(bf16[256,640]{1,0:T(8,128)(2,1)} %add_convert_fusion.2), channel_id=1, source_target_pairs={{0,1},{1,0},{2,3},{3,2},{4,5},{5,4},{6,7},{7,6},{8,9},{9,8},{10,11... | collective-permute-start | bytes 983048 | tf_op jit(solution)/shard_map/ppermute | solution.py:39
  381.9 24.9 %collective-permute-start.55 = (bf16[320,640]{1,0:T(8,128)(2,1)S(1)}, bf16[320,640]{1,0:T(8,128)(2,1)}, u32[]{:S(2)}, u32[]{:S(2)}) collective-permute-start(bf16[320,640]{1,0:T(8,128)(2,1)S(1)} %slice.267), channel_id=1, source_target_pairs={{0,2},{2,0},{1,3},{3,1},{4,6},{6,4},{5,7},{7,5},{8,10},{10,8},{9,1... | collective-permute-start | bytes 1228808 | tf_op jit(solution)/shard_map/ppermute | solution.py:39
  387.2 18.9 %all-to-all-start.6 = ((bf16[4,160,640]{2,1,0:T(8,128)(2,1)}), bf16[4,160,640]{2,1,0:T(8,128)(2,1)S(1)}, u32[]{:S(2)}, u32[]{:S(2)}) async-start(bf16[4,160,640]{2,1,0:T(8,128)(2,1)} %bitcast.34), calls=%async_computation.6 | async-start | bytes 1638400 | tf_op jit(solution)/shard_map/all_to_all | solution.py:152
  420.7 35.7 %all-to-all-start.7 = ((bf16[4,512,640]{2,1,0:T(8,128)(2,1)}), bf16[4,512,640]{2,1,0:T(8,128)(2,1)}, u32[]{:S(2)}, u32[]{:S(2)}) async-start(bf16[4,512,640]{2,1,0:T(8,128)(2,1)} %broadcast_in_dim.70), calls=%async_computation.7 | async-start | bytes 5242880 | tf_op jit(solution)/shard_map/all_to_all | solution.py:152
  459.3 33.3 %all-to-all-start.8 = ((bf16[4,480,640]{2,1,0:T(8,128)(2,1)}), bf16[4,480,640]{2,1,0:T(8,128)(2,1)S(1)}, u32[]{:S(2)}, u32[]{:S(2)}) async-start(bf16[4,480,640]{2,1,0:T(8,128)(2,1)} %broadcast_in_dim.73), calls=%async_computation.8 | async-start | bytes 4915200 | tf_op jit(solution)/shard_map/all_to_all | solution.py:152
  (118 other events, 1090.6 us)
where the time goes:
time: 519 us; the launch traced here: 509 us
  waiting for transfers between devices  157 us (30%)
  Pallas kernels  115 us (22%)
  starting transfers between devices  101 us (19%)
  matrix products  57.9 us (11%)
  other arithmetic  42.8 us (8%)
  local copies, waits for them, and re-layouts  30.6 us (6%)
    ppermute x58, waiting for transfers between devices, flip(): return lax.ppermute(x, axis, FLIP)  110 us
    ppermute x58, starting transfers between devices, flip(): return lax.ppermute(x, axis, FLIP)  47.3 us
    all_to_all x9, waiting for transfers between devices, exchange_rest(): return lax.all_to_all(x, 'r', 0, 0)  47.3 us
    pallas_call x2, Pallas kernels, attend_backward(): pl.pallas_call(kernel, grid=(4,), in_specs=[whole(rows, width3), pl.Block...  45.9 us
    dot_general x23, matrix products, dot(): return jnp.dot(left, right, preferred_element_type=F32)  40.8 us
    all_to_all x9, starting transfers between devices, exchange_rest(): return lax.all_to_all(x, 'r', 0, 0)  39 us
    pallas_call x2, Pallas kernels, attend_forward(): pl.pallas_call(functools.partial(attend_forward_kernel, heads), grid=(2,)...  28 us
    dot_general x16, matrix products, dot_nt(): lax.dot_general(left, right, (((1,), (1,)), ((), ())), preferred_element_...  17.1 us
  transfers between devices with their start and end apart: 73, of which 29 were waited for; matrix products, arithmetic and copies ran while one was open for 21% of the time, Pallas kernels for 22%

commit v1 on v0

--- a/solution.py
+++ b/solution.py
@@ -423,7 +423,11 @@
         p_scr[:, cols] = probs.astype(BF)
         ds = (probs * (dot_nt(v_scr[...], do_head) - inner[h : h + 1, :])).astype(BF)
         ds_scr[:, cols] = ds
-        dqt_scr[h * HD : (h + 1) * HD, :] = dot(kt_scr[h * HD : (h + 1) * HD, :], ds) * scale
+    wide = dot(kt_scr[...], ds_scr[...])
+    for h in range(heads):
+        dqt_scr[h * HD : (h + 1) * HD, :] = (
+            wide[h * HD : (h + 1) * HD, h * blk : (h + 1) * blk] * scale
+        )
     dv_scr[...] += dot(p_scr[...], doh_scr[...])
     dk_scr[...] += dot(ds_scr[...], qh_scr[...])
     grad_ref[rows, :width] = dqt_scr[...].T.astype(BF)
@@ -571,11 +575,11 @@
         else:
             mix_w, out_w = attn_weights(1, tie(attn_1, normed))
         if first:
-            shadow = far_0 = flip(tie(far_ffn(0), normed), "zh")
+            far_0 = tie(far_ffn(0), normed)
+            attn_blocks = tie(attn_blocks, far_0)
+            shadow = far_0 = flip(far_0, "zh")
         else:
-            far_1 = flip(tie(far_ffn(1), normed), "zh")
-            down_blocks = gather_start(tie(cotangent_home, normed))
-            shadow = far_1, down_blocks
+            shadow = far_1 = flip(tie(far_ffn(1), attn_blocks[2]), "zh")
         *attn_parts, x, mixed, attended, log_totals = tie(
             attend_forward(attn_blocks, mix_w, bias, out_w), shadow
         )
@@ -595,12 +599,15 @@
             up_w, down_w = ffn_weights(depth, tie(far_0, normed_two))
         else:
             up_w, down_w = ffn_weights(depth, tie(far_1, normed_two))
+        ffn_blocks = tie(ffn_blocks, up_w, down_w)
+        if last:
+            down_blocks = gather_start(tie(cotangent_home, ffn_blocks[2]))
         ffn_outs, acts, us = zip(*(ffn_forward(b, up_w, down_w) for b in ffn_blocks))
         own, core, plane, both = ffn_outs
         if first:
             plane, both = tie((plane, both), attn_1, cotangent_home)
-            attn_1 = spread_rest(attn_1, rest)
             sent, came = scatter_far(plane, both)
+            attn_1 = spread_rest(tie(attn_1, sent), rest)
             parts = (own, flip(core, "c"), came)
         saved.append(
             dict(
@@ -623,18 +630,21 @@
         left, right = (jnp.concatenate(x, axis=0) for x in (left, right))
         return dot(left.T, right).astype(BF)
 
-    def ffn_blocks_backward(keep, blocks, before=()):
+    def ffn_blocks_backward(keep, blocks):
         _, _, up_w, down_w = keep["weights"]
         outs, pres = [None] * 4, [None] * 4
         for k in (3, 2):
             outs[k], pres[k] = ffn_backward(blocks[k], up_w, down_w, keep["u"][k])
-        sent, came = scatter_far(*tie(outs[2:], before))
+        sent, came = scatter_far(*outs[2:])
         for k in (1, 0):
             outs[k], pres[k] = ffn_backward(blocks[k], up_w, down_w, keep["u"][k])
         parts = (outs[0], flip(outs[1], "c"), came)
-        grad_down = transposed_dot(tie(keep["act"], sent), blocks)
-        grad_up = transposed_dot(tie(keep["ffn"], sent), pres)
-        return parts, sent, ffn_grad_rows(grad_up, grad_down)
+        return parts, sent, pres
+
+    def ffn_weight_grads(keep, blocks, pres, after):
+        grad_down = transposed_dot(tie(keep["act"], after), blocks)
+        grad_up = transposed_dot(tie(keep["ffn"], after), pres)
+        return ffn_grad_rows(grad_up, grad_down)
 
     def ffn_grad_rows(grad_up, grad_down):
         rows = [
@@ -660,10 +670,9 @@
         rows = jnp.concatenate([grad_mix.astype(BF), grad_out.astype(BF)], axis=0)
         return rows.reshape(rest, slab_attn, model_width)
 
-    def finish_attn(mine, other):
-        sums = jnp.where(
-            at_home, mine[:, span : span + slab_attn], other[:, span : span + slab_attn]
-        )
+    def finish_attn(mine, other, first):
+        end = first + slab_attn
+        sums = jnp.where(at_home, mine[:, first:end], other[:, first:end])
         sums = sums.reshape(4 * local_width, model_width)
         mix = sums[: 3 * local_width].reshape(3, local_width, model_width)
         return mix.astype(F32), sums[3 * local_width :].astype(F32)
@@ -681,8 +690,8 @@
         return jnp.sum(x.astype(F32), axis=0)
 
     keep = saved[1]
-    parts, sent, ffn_a = ffn_blocks_backward(keep, down_blocks)
-    ffn_a = exchange_rest(ffn_a)
+    parts, sent, pres = ffn_blocks_backward(keep, down_blocks)
+    ffn_a = exchange_rest(ffn_weight_grads(keep, down_blocks, pres, sent))
     grad, low, sums_11 = norm_backward(parts, keep["middle"], cotangent_home, ln_gain[1, 1])
     row_blocks = gather_start(low)
 
@@ -692,7 +701,6 @@
     *parts, mix_grad, grad_out = tie(attn_backward(keep, row_blocks), plane, core, ffn_a)
     sent, came = scatter_far(*parts[2:])
     parts = (parts[0], flip(parts[1], "c"), came)
-    ffn_a = sum_first(tie(ffn_a, sent)).astype(BF)
     grad_mix = dot(tie(mix_grad, sent).T, keep["x"])
     attn_a = attn_grad_rows(grad_mix, grad_out)
     grad, low, sums_10 = norm_backward(parts, keep["entry"], grad, ln_gain[1, 0])
@@ -700,7 +708,8 @@
 
     down_blocks = gather_start(low)
     keep = saved[0]
-    parts, sent, ffn_b = ffn_blocks_backward(keep, down_blocks)
+    parts, sent, pres = ffn_blocks_backward(keep, down_blocks)
+    ffn_b = ffn_weight_grads(keep, down_blocks, pres, sent)
     attn_a = sum_first(tie(attn_a, sent)).astype(BF)
     parts, ffn_b = tie((parts, ffn_b), attn_a)
     ffn_b = exchange_rest(ffn_b)
@@ -708,6 +717,7 @@
     row_blocks = gather_start(low)
     plane, core = tie((plane, core), low)
     final = saved[1]["middle"] + own.astype(F32) + core.astype(F32) + plane.astype(F32)
+    ffn_a = sum_first(tie(ffn_a, low)).astype(BF)
     held = jnp.concatenate([ffn_a[span:], attn_a], axis=0)
     came_a = flip(tie(held, low), "zh")
 
@@ -718,6 +728,7 @@
     came_b = flip(ffn_b[span:].astype(BF), "zh")
     grad_mix = dot(tie(mix_grad, sent).T, keep["x"])
     attn_b = exchange_rest(attn_grad_rows(grad_mix, grad_out))
+    parts = tie(parts, came_b)
     grad, low, sums_00 = norm_backward(parts, keep["entry"], grad, ln_gain[0, 0])
 
     first_of_four = (zh == 0) & (zl == 0)
@@ -745,16 +756,17 @@
     attn_b = sum_first(tie(attn_b, low)).astype(BF)
     sent_c = jnp.concatenate([attn_b, in_two(small)], axis=0)
     came_c = flip(sent_c, "zh")
+    rows_b = spread_rest((ffn_b[:span] + came_b.astype(F32)).astype(BF), rest)
     small = small + from_two(came_c[slab_attn:])
-    rows_b = jnp.concatenate(
+    rows_a = jnp.concatenate(
         [
-            (ffn_b[:span] + came_b.astype(F32)).astype(BF),
+            added(jnp.concatenate([ffn_a[:span], attn_a], axis=0), tie(came_a, sent)),
             added(attn_b, came_c[:slab_attn]),
             in_two(small),
         ],
         axis=0,
     )
-    rows_b = spread_rest(rows_b, rest)
+    rows_a = spread_rest(tie(rows_a, rows_b), rest)
     layer_out = rehome(tie(final.astype(BF), low))
     grad_tokens = rehome(low)
     row_ids = (2 * zh + zl) * rows_shard + jnp.arange(rows_shard, dtype=jnp.int32)
@@ -766,19 +778,15 @@
     picked = jnp.sum(jnp.where(labels[:, None] == classes[None, :], logits, 0.0), axis=-1)
     label_logprob = jnp.where(live_rows, picked - log_total, jnp.zeros_like(log_total))
 
-    rows_a = added(jnp.concatenate([ffn_a[:span], attn_a], axis=0), came_a)
-    rows_a = spread_rest(tie(rows_a, rows_b), rest)
-    rows_b, layer_out, label_logprob, grad_tokens = tie(
-        (rows_b, layer_out, label_logprob, grad_tokens)
-    )
     rows_b = (rows_b, flip(rows_b, "c"))
     ffn_stacks = finish_ffn(0, *rows_b, None)
-    attn_b = finish_attn(*rows_b)
-    small = sum(jnp.sum(from_two(x[:, span + slab_attn :]), axis=0) for x in rows_b)
-    rows_a, ffn_stacks, attn_b, small = tie((rows_a, ffn_stacks, attn_b, small))
+    rows_a, ffn_stacks, layer_out, label_logprob, grad_tokens = tie(
+        (rows_a, ffn_stacks, layer_out, label_logprob, grad_tokens)
+    )
     rows_a = (rows_a, flip(rows_a, "c"))
+    small = sum(jnp.sum(from_two(x[:, span + 2 * slab_attn :]), axis=0) for x in rows_a)
     grads_up, grads_down = finish_ffn(1, *rows_a, ffn_stacks)
-    attn_a = finish_attn(*rows_a)
+    attn_a, attn_b = (finish_attn(*rows_a, span + k * slab_attn) for k in (0, 1))
     grads_mix, grads_out = (jnp.stack(pair) for pair in zip(attn_b, attn_a))
     grads_mix = jnp.transpose(grads_mix, (0, 3, 1, 2))
     grad_tokens = grad_tokens.astype(F32)

time: 519 us -> 492 us (0.948)
  waiting for transfers between devices: 157 us -> 133 us
  other arithmetic: 42.8 us -> 35.8 us
  starting transfers between devices: 101 us -> 107 us
    all_to_all x9, waiting for transfers between devices: 47.3 us -> 29.8 us  [exchange_rest(): return lax.all_to_all(x, 'r', 0, 0)]
    ppermute x58, waiting for transfers between devices: 110 us -> 103 us  [flip(): return lax.ppermute(x, axis, FLIP)]
    ppermute x58, starting transfers between devices: 47.3 us -> 53.4 us  [flip(): return lax.ppermute(x, axis, FLIP)]
    unnamed x157 -> x141, local copies, waits for them, and re-layouts: 10.7 us -> 12.4 us
  transfers between devices with their start and end apart: 73 -> 73, of which waited for: 29 -> 30; matrix products, arithmetic and copies ran while one was open for 21% -> 21% of each run, Pallas kernels for 22% -> 22%
where the time goes in v1:
time: 492 us; the launch traced here: 482 us
  waiting for transfers between devices  133 us (27%)
  Pallas kernels  111 us (23%)
  starting transfers between devices  107 us (22%)
  matrix products  58.8 us (12%)
  other arithmetic  35.8 us (7%)
  local copies, waits for them, and re-layouts  32.8 us (7%)
    ppermute x58, waiting for transfers between devices, flip(): return lax.ppermute(x, axis, FLIP)  103 us
    ppermute x58, starting transfers between devices, flip(): return lax.ppermute(x, axis, FLIP)  53.4 us
    pallas_call x2, Pallas kernels, attend_backward(): pl.pallas_call(kernel, grid=(4,), in_specs=[whole(rows, width3), pl.Block...  41.3 us
    dot_general x23, matrix products, dot(): return jnp.dot(left, right, preferred_element_type=F32)  40.1 us
    all_to_all x9, starting transfers between devices, exchange_rest(): return lax.all_to_all(x, 'r', 0, 0)  37.6 us
    all_to_all x9, waiting for transfers between devices, exchange_rest(): return lax.all_to_all(x, 'r', 0, 0)  29.8 us
    pallas_call x2, Pallas kernels, attend_forward(): pl.pallas_call(functools.partial(attend_forward_kernel, heads), grid=(2,)...  28 us
    dot_general x16, matrix products, dot_nt(): lax.dot_general(left, right, (((1,), (1,)), ((), ())), preferred_element_...  18.7 us
  transfers between devices with their start and end apart: 73, of which 30 were waited for; matrix products, arithmetic and copies ran while one was open for 21% of the time, Pallas kernels for 22%

profile of v1, /device:TPU:0, one launch (start us, length us, event | category | flops | bytes accessed | tf_op | source)
XLA Modules:
  0.0 482.2 jit_solution(8127731043024110148)
XLA Ops:
  18.9 7.0 %collective-permute-start.2 = (bf16[256,640]{1,0:T(8,128)(2,1)}, bf16[256,640]{1,0:T(8,128)(2,1)}, u32[]{:S(2)}, u32[]{:S(2)}) collective-permute-start(bf16[256,640]{1,0:T(8,128)(2,1)} %get-tuple-element.168.own_x_ref), channel_id=1, source_target_pairs={{0,4},{4,0},{1,5},{5,1},{2,6},{6,2},{3,7},{7,3},{8,12},{12,8},{9,1... | collective-permute-start | bytes 983048 | tf_op jit(solution)/shard_map/ppermute | solution.py:39
  25.9 8.9 %collective-permute-start.4 = (bf16[256,640]{1,0:T(8,128)(2,1)}, bf16[256,640]{1,0:T(8,128)(2,1)}, u32[]{:S(2)}, u32[]{:S(2)}) collective-permute-start(bf16[256,640]{1,0:T(8,128)(2,1)} %collective-permute-done.3.plane_x_ref), channel_id=1, source_target_pairs={{0,4},{4,0},{1,5},{5,1},{2,6},{6,2},{3,7},{7,3},{8,12},{12,8},{9,1... | collective-permute-start | bytes 983048 | tf_op jit(solution)/shard_map/ppermute | solution.py:39
  41.7 14.0 %attend_forward.2 = (bf16[256,640]{1,0:T(8,128)(2,1)}, bf16[256,640]{1,0:T(8,128)(2,1)}, bf16[256,640]{1,0:T(8,128)(2,1)}, bf16[256,640]{1,0:T(8,128)(2,1)}, bf1...) custom-call(bf16[256,640]{1,0:T(8,128)(2,1)} %get-tuple-element.168.own_x_ref, ...), custom_call_target="tpu_custom_call" | custom-call | flops 4600000000 | bytes 1048576 | tf_op jit(solution)/shard_map/attend_forward/pallas_call | solution.py:326
  55.6 4.3 collective-permute-done.7
  69.6 8.5 %collective-permute-done.10.refs_2_ = bf16[256,640]{1,0:T(8,128)(2,1)S(1)} collective-permute-done((bf16[256,640]{1,0:T(8,128)(2,1)S(1)}, bf16[256,640]{1,0:T(8,128)(2,1)S(1)}, u32[]{:S(2)}, u32[]{:S(2)}) %collective-permute-start.10) | collective-permute-done | bytes 327712 | tf_op jit(solution)/shard_map/ppermute | solution.py:39
  86.3 4.1 collective-permute-start.16
  90.3 5.4 %collective-permute-done.12 = bf16[256,640]{1,0:T(8,128)(2,1)S(1)} collective-permute-done((bf16[256,640]{1,0:T(8,128)(2,1)}, bf16[256,640]{1,0:T(8,128)(2,1)S(1)}, u32[]{:S(2)}, u32[]{:S(2)}) %collective-permute-start.12) | collective-permute-done | bytes 327712 | tf_op jit(solution)/shard_map/ppermute | solution.py:39
  97.0 4.3 ffn_weights_here.2
  115.0 4.3 all-to-all-start.1
  140.5 14.0 %attend_forward.3 = (bf16[256,640]{1,0:T(8,128)(2,1)}, bf16[256,640]{1,0:T(8,128)(2,1)}, bf16[256,640]{1,0:T(8,128)(2,1)}, bf16[256,640]{1,0:T(8,128)(2,1)}, bf1...) custom-call(bf16[256,640]{1,0:T(8,128)(2,1)} %get-tuple-element.199.own_x_ref, ...), custom_call_target="tpu_custom_call" | custom-call | flops 4600000000 | bytes 1048576 | tf_op jit(solution)/shard_map/attend_forward/pallas_call | solution.py:326
  154.5 4.1 collective-permute-done.22
  169.3 8.5 %collective-permute-done.25.refs_2_ = bf16[256,640]{1,0:T(8,128)(2,1)S(1)} collective-permute-done((bf16[256,640]{1,0:T(8,128)(2,1)}, bf16[256,640]{1,0:T(8,128)(2,1)S(1)}, u32[]{:S(2)}, u32[]{:S(2)}) %collective-permute-start.25) | collective-permute-done | bytes 327712 | tf_op jit(solution)/shard_map/ppermute | solution.py:39
  181.3 9.4 %collective-permute-done.27 = bf16[256,640]{1,0:T(8,128)(2,1)} collective-permute-done((bf16[256,640]{1,0:T(8,128)(2,1)}, bf16[256,640]{1,0:T(8,128)(2,1)}, u32[]{:S(2)}, u32[]{:S(2)}) %collective-permute-start.27) | collective-permute-done | bytes 327712 | tf_op jit(solution)/shard_map/ppermute | solution.py:39
  191.9 4.7 ffn_weights_here.3
  225.8 4.9 %all-to-all-start.3 = ((bf16[4,640,640]{2,1,0:T(8,128)(2,1)}), bf16[4,640,640]{2,1,0:T(8,128)(2,1)}, u32[]{:S(2)}, u32[]{:S(2)}) async-start(bf16[4,640,640]{2,1,0:T(8,128)(2,1)} %pad_maximum_fusion), calls=%async_computation.3 | async-start | bytes 6553600 | tf_op jit(solution)/shard_map/all_to_all | solution.py:152
  237.4 6.9 %collective-permute-done.36.refs_6_ = bf16[256,640]{1,0:T(8,128)(2,1)S(1)} collective-permute-done((bf16[256,640]{1,0:T(8,128)(2,1)}, bf16[256,640]{1,0:T(8,128)(2,1)S(1)}, u32[]{:S(2)}, u32[]{:S(2)}) %collective-permute-start.36) | collective-permute-done | bytes 327712 | tf_op jit(solution)/shard_map/ppermute | solution.py:39
  248.1 20.6 %attend_backward.2 = (bf16[256,640]{1,0:T(8,128)(2,1)}, bf16[256,640]{1,0:T(8,128)(2,1)}, bf16[256,640]{1,0:T(8,128)(2,1)}, bf16[256,640]{1,0:T(8,128)(2,1)}, bf...) custom-call(bf16[1024,480]{1,0:T(8,128)(2,1)} %get-tuple-element.233.refs_0_, f32[1024,1024]{1,0:T(8,128)} %fusion.1.bias_ref.refs_1_, ...), custom_call_target="tpu_custom_call" | custom-call | flops 6899999744 | bytes 1048576 | tf_op jit(solution)/shard_map/attend_backward/pallas_call | solution.py:454
  277.0 4.4 all-to-all-start.4
  290.5 4.7 collective-permute-done.46
  312.9 4.4 all-to-all-start.5
  325.1 4.3 collective-permute-done.52.refs_6_
  334.2 20.6 %attend_backward.3 = (bf16[256,640]{1,0:T(8,128)(2,1)}, bf16[256,640]{1,0:T(8,128)(2,1)}, bf16[256,640]{1,0:T(8,128)(2,1)}, bf16[256,640]{1,0:T(8,128)(2,1)}, bf...) custom-call(bf16[1024,480]{1,0:T(8,128)(2,1)} %get-tuple-element.273.refs_0_, f32[1024,1024]{1,0:T(8,128)} %fusion.1.bias_ref.refs_1_, ...), custom_call_target="tpu_custom_call" | custom-call | flops 6899999744 | bytes 1048576 | tf_op jit(solution)/shard_map/attend_backward/pallas_call | solution.py:454
  354.8 7.1 %collective-permute-done.50 = bf16[480,640]{1,0:T(8,128)(2,1)} collective-permute-done((bf16[480,640]{1,0:T(8,128)(2,1)S(1)}, bf16[480,640]{1,0:T(8,128)(2,1)}, u32[]{:S(2)}, u32[]{:S(2)}) %collective-permute-start.50) | collective-permute-done | bytes 614432 | tf_op jit(solution)/shard_map/ppermute | solution.py:39
  371.2 4.0 all-to-all-start.6
  375.2 7.0 %collective-permute-done.56.plane_ref = bf16[256,640]{1,0:T(8,128)(2,1)} collective-permute-done((bf16[256,640]{1,0:T(8,128)(2,1)}, bf16[256,640]{1,0:T(8,128)(2,1)}, u32[]{:S(2)}, u32[]{:S(2)}) %collective-permute-start.56) | collective-permute-done | bytes 327712 | tf_op jit(solution)/shard_map/ppermute | solution.py:39
  382.2 5.4 %collective-permute-done.57 = bf16[320,640]{1,0:T(8,128)(2,1)S(1)} collective-permute-done((bf16[320,640]{1,0:T(8,128)(2,1)S(1)}, bf16[320,640]{1,0:T(8,128)(2,1)S(1)}, u32[]{:S(2)}, u32[]{:S(2)}) %collective-permute-start.57) | collective-permute-done | bytes 409632 | tf_op jit(solution)/shard_map/ppermute | solution.py:39
  393.1 4.1 all-to-all-start.7
  401.6 8.9 %collective-permute-done.59 = bf16[192,640]{1,0:T(8,128)(2,1)S(1)} collective-permute-done((bf16[192,640]{1,0:T(8,128)(2,1)S(1)}, bf16[192,640]{1,0:T(8,128)(2,1)S(1)}, u32[]{:S(2)}, u32[]{:S(2)}) %collective-permute-start.59) | collective-permute-done | bytes 245792 | tf_op jit(solution)/shard_map/ppermute | solution.py:39
  410.8 5.8 %all-to-all-done.7.mine_ref = bf16[4,320,640]{2,1,0:T(8,128)(2,1)S(1)} async-done(((bf16[4,320,640]{2,1,0:T(8,128)(2,1)}), bf16[4,320,640]{2,1,0:T(8,128)(2,1)S(1)}, u32[]{:S(2)}, u32[]{:S(2)}) %all-to-all-start.7) | async-done | bytes 1638432 | tf_op jit(solution)/shard_map/all_to_all | solution.py:152
  434.6 5.1 %ffn_grads.2 = (f32[2,640,1280]{2,1,0:T(8,128)}, f32[2,2,640,640]{3,2,1,0:T(8,128)}) custom-call(s32[1]{0:T(128)} %bitcast.11.place_ref, bf16[4,320,640]{2,1,0:T(8,128)(2,1)} %copy-done.10, bf16[4,320,640]{2,1,0:T(8,128)(2,1)} %collective-permute-done.60.other_ref), custom_call_target="tpu_custom_call" | custom-call | flops 4600000000 | bytes 1048576 | tf_op jit(solution)/shard_map/ffn_grads/pallas_call | solution.py:225
  439.7 21.6 %all-to-all-done.8.mine_ref = bf16[4,672,640]{2,1,0:T(8,128)(2,1)S(1)} async-done(((bf16[4,672,640]{2,1,0:T(8,128)(2,1)}), bf16[4,672,640]{2,1,0:T(8,128)(2,1)S(1)}, u32[]{:S(2)}, u32[]{:S(2)}) %all-to-all-start.8) | async-done | bytes 3440672 | tf_op jit(solution)/shard_map/all_to_all | solution.py:152
  473.8 5.1 %ffn_grads.3 = (f32[2,640,1280]{2,1,0:T(8,128)}, f32[2,2,640,640]{3,2,1,0:T(8,128)}) custom-call(s32[1]{0:T(128)} %bitcast.11.place_ref, bf16[4,672,640]{2,1,0:T(8,128)(2,1)} %copy-done.3, bf16[4,672,640]{2,1,0:T(8,128)(2,1)} %copy-done.4, f32[2,640,1280]{2,1,0:T(8,128)} %get-tuple-element.313.refs_0_, ...), custom_call_target="tpu_custom_call", output_to_operand_aliasing={{0}: (3, {}), {1}: (4, {})} | custom-call | flops 4600000000 | bytes 1048576 | tf_op jit(solution)/shard_map/ffn_grads/pallas_call | solution.py:225
  (394 shorter events, 231.1 us)
Async XLA Ops:
  5.2 35.7 %collective-permute-start.6 = (bf16[160,640]{1,0:T(8,128)(2,1)S(1)}, bf16[160,640]{1,0:T(8,128)(2,1)S(1)}, u32[]{:S(2)}, u32[]{:S(2)}) collective-permute-start(bf16[160,640]{1,0:T(8,128)(2,1)S(1)} %get-tuple-element.339), channel_id=1, source_target_pairs={{0,0},{1,1},{2,4},{3,5},{4,2},{5,3},{6,6},{7,7},{8,8},{9,9},{10,12... | collective-permute-start | bytes 614408 | tf_op jit(solution)/shard_map/ppermute | solution.py:35
  7.3 33.7 %collective-permute-start.5 = (bf16[480,640]{1,0:T(8,128)(2,1)S(1)}, bf16[480,640]{1,0:T(8,128)(2,1)}, u32[]{:S(2)}, u32[]{:S(2)}) collective-permute-start(bf16[480,640]{1,0:T(8,128)(2,1)S(1)} %bitcast.161), channel_id=1, source_target_pairs={{0,0},{1,1},{2,4},{3,5},{4,2},{5,3},{6,6},{7,7},{8,8},{9,9},{10,12... | collective-permute-start | bytes 1843208 | tf_op jit(solution)/shard_map/ppermute | solution.py:35
  18.9 22.1 %collective-permute-start.2 = (bf16[256,640]{1,0:T(8,128)(2,1)}, bf16[256,640]{1,0:T(8,128)(2,1)}, u32[]{:S(2)}, u32[]{:S(2)}) collective-permute-start(bf16[256,640]{1,0:T(8,128)(2,1)} %get-tuple-element.168.own_x_ref), channel_id=1, source_target_pairs={{0,4},{4,0},{1,5},{5,1},{2,6},{6,2},{3,7},{7,3},{8,12},{12,8},{9,1... | collective-permute-start | bytes 983048 | tf_op jit(solution)/shard_map/ppermute | solution.py:39
  25.9 15.1 %collective-permute-start.4 = (bf16[256,640]{1,0:T(8,128)(2,1)}, bf16[256,640]{1,0:T(8,128)(2,1)}, u32[]{:S(2)}, u32[]{:S(2)}) collective-permute-start(bf16[256,640]{1,0:T(8,128)(2,1)} %collective-permute-done.3.plane_x_ref), channel_id=1, source_target_pairs={{0,4},{4,0},{1,5},{5,1},{2,6},{6,2},{3,7},{7,3},{8,12},{12,8},{9,1... | collective-permute-start | bytes 983048 | tf_op jit(solution)/shard_map/ppermute | solution.py:39
  37.8 22.1 %collective-permute-start.7 = (bf16[320,640]{1,0:T(8,128)(2,1)S(1)}, bf16[320,640]{1,0:T(8,128)(2,1)S(1)}, u32[]{:S(2)}, u32[]{:S(2)}) collective-permute-start(bf16[320,640]{1,0:T(8,128)(2,1)S(1)} %pad_maximum_fusion.7), channel_id=1, source_target_pairs={{0,2},{2,0},{1,3},{3,1},{4,6},{6,4},{5,7},{7,5},{8,10},{10,8},{9,1... | collective-permute-start | bytes 1228808 | tf_op jit(solution)/shard_map/ppermute | solution.py:39
  64.1 31.7 %all-to-all-start = ((bf16[4,320,640]{2,1,0:T(8,128)(2,1)}), bf16[4,320,640]{2,1,0:T(8,128)(2,1)S(1)}, u32[]{:S(2)}, u32[]{:S(2)}) async-start(bf16[4,320,640]{2,1,0:T(8,128)(2,1)} %broadcast_in_dim.32), calls=%async_computation | async-start | bytes 3276800 | tf_op jit(solution)/shard_map/all_to_all | solution.py:152
  81.3 14.5 %collective-permute-start.12 = (bf16[256,640]{1,0:T(8,128)(2,1)}, bf16[256,640]{1,0:T(8,128)(2,1)S(1)}, u32[]{:S(2)}, u32[]{:S(2)}) collective-permute-start(bf16[256,640]{1,0:T(8,128)(2,1)} %get-tuple-element.253), channel_id=1, source_target_pairs={{0,1},{1,0},{2,3},{3,2},{4,5},{5,4},{6,7},{7,6},{8,9},{9,8},{10,11... | collective-permute-start | bytes 983048 | tf_op jit(solution)/shard_map/ppermute | solution.py:39
  82.9 25.1 %collective-permute-start.15 = (bf16[160,640]{1,0:T(8,128)(2,1)}, bf16[160,640]{1,0:T(8,128)(2,1)S(1)}, u32[]{:S(2)}, u32[]{:S(2)}) collective-permute-start(bf16[160,640]{1,0:T(8,128)(2,1)} %fusion.101), channel_id=1, source_target_pairs={{0,2},{2,0},{1,3},{3,1},{4,6},{6,4},{5,7},{7,5},{8,10},{10,8},{9,1... | collective-permute-start | bytes 614408 | tf_op jit(solution)/shard_map/ppermute | solution.py:39
  86.3 15.1 %collective-permute-start.11 = (bf16[256,640]{1,0:T(8,128)(2,1)}, bf16[256,640]{1,0:T(8,128)(2,1)S(1)}, u32[]{:S(2)}, u32[]{:S(2)}) collective-permute-start(bf16[256,640]{1,0:T(8,128)(2,1)} %get-tuple-element.253), channel_id=1, source_target_pairs={{0,4},{4,0},{1,5},{5,1},{2,6},{6,2},{3,7},{7,3},{8,12},{12,8},{9,1... | collective-permute-start | bytes 983048 | tf_op jit(solution)/shard_map/ppermute | solution.py:39
  86.3 21.8 %collective-permute-start.16 = (bf16[256,640]{1,0:T(8,128)(2,1)}, bf16[256,640]{1,0:T(8,128)(2,1)}, u32[]{:S(2)}, u32[]{:S(2)}) collective-permute-start(bf16[256,640]{1,0:T(8,128)(2,1)} %param.23), channel_id=1, source_target_pairs={{0,0},{1,1},{2,4},{3,5},{4,2},{5,3},{6,6},{7,7},{8,8},{9,9},{10,12... | collective-permute-start | bytes 983048 | tf_op jit(solution)/shard_map/ppermute | solution.py:35
  115.0 16.1 %all-to-all-start.1 = ((bf16[4,160,640]{2,1,0:T(8,128)(2,1)}), bf16[4,160,640]{2,1,0:T(8,128)(2,1)S(1)}, u32[]{:S(2)}, u32[]{:S(2)}) async-start(bf16[4,160,640]{2,1,0:T(8,128)(2,1)} %broadcast_in_dim.33), calls=%async_computation.1 | async-start | bytes 1638400 | tf_op jit(solution)/shard_map/all_to_all | solution.py:152
  136.8 21.9 %collective-permute-start.22 = (bf16[320,640]{1,0:T(8,128)(2,1)S(1)}, bf16[320,640]{1,0:T(8,128)(2,1)S(1)}, u32[]{:S(2)}, u32[]{:S(2)}) collective-permute-start(bf16[320,640]{1,0:T(8,128)(2,1)S(1)} %copy-done.29), channel_id=1, source_target_pairs={{0,2},{2,0},{1,3},{3,1},{4,6},{6,4},{5,7},{7,5},{8,10},{10,8},{9,1... | collective-permute-start | bytes 1228808 | tf_op jit(solution)/shard_map/ppermute | solution.py:39
  163.6 27.1 %all-to-all-start.2 = ((bf16[4,320,640]{2,1,0:T(8,128)(2,1)}), bf16[4,320,640]{2,1,0:T(8,128)(2,1)S(1)}, u32[]{:S(2)}, u32[]{:S(2)}) async-start(bf16[4,320,640]{2,1,0:T(8,128)(2,1)} %broadcast_in_dim.34), calls=%async_computation.2 | async-start | bytes 3276800 | tf_op jit(solution)/shard_map/all_to_all | solution.py:152
  181.3 15.3 %collective-permute-start.26 = (bf16[256,640]{1,0:T(8,128)(2,1)}, bf16[256,640]{1,0:T(8,128)(2,1)}, u32[]{:S(2)}, u32[]{:S(2)}) collective-permute-start(bf16[256,640]{1,0:T(8,128)(2,1)} %get-tuple-element.225), channel_id=1, source_target_pairs={{0,4},{4,0},{1,5},{5,1},{2,6},{6,2},{3,7},{7,3},{8,12},{12,8},{9,1... | collective-permute-start | bytes 983048 | tf_op jit(solution)/shard_map/ppermute | solution.py:39
  210.5 20.2 %collective-permute-start.33 = (bf16[256,640]{1,0:T(8,128)(2,1)}, bf16[256,640]{1,0:T(8,128)(2,1)S(1)}, u32[]{:S(2)}, u32[]{:S(2)}) collective-permute-start(bf16[256,640]{1,0:T(8,128)(2,1)} %convolution_convert_fusion.14), channel_id=1, source_target_pairs={{0,4},{4,0},{1,5},{5,1},{2,6},{6,2},{3,7},{7,3},{8,12},{12,8},{9,1... | collective-permute-start | bytes 983048 | tf_op jit(solution)/shard_map/ppermute | solution.py:39
  215.6 15.1 %collective-permute-start.34 = (bf16[256,640]{1,0:T(8,128)(2,1)}, bf16[256,640]{1,0:T(8,128)(2,1)}, u32[]{:S(2)}, u32[]{:S(2)}) collective-permute-start(bf16[256,640]{1,0:T(8,128)(2,1)} %add_convert_fusion.6), channel_id=1, source_target_pairs={{0,1},{1,0},{2,3},{3,2},{4,5},{5,4},{6,7},{7,6},{8,9},{9,8},{10,11... | collective-permute-start | bytes 983048 | tf_op jit(solution)/shard_map/ppermute | solution.py:39
  225.8 43.0 %all-to-all-start.3 = ((bf16[4,640,640]{2,1,0:T(8,128)(2,1)}), bf16[4,640,640]{2,1,0:T(8,128)(2,1)}, u32[]{:S(2)}, u32[]{:S(2)}) async-start(bf16[4,640,640]{2,1,0:T(8,128)(2,1)} %pad_maximum_fusion), calls=%async_computation.3 | async-start | bytes 6553600 | tf_op jit(solution)/shard_map/all_to_all | solution.py:152
  246.3 22.5 %collective-permute-start.40 = (bf16[256,640]{1,0:T(8,128)(2,1)S(1)}, bf16[256,640]{1,0:T(8,128)(2,1)}, u32[]{:S(2)}, u32[]{:S(2)}) collective-permute-start(bf16[256,640]{1,0:T(8,128)(2,1)S(1)} %convolution_convert_fusion.12), channel_id=1, source_target_pairs={{0,4},{4,0},{1,5},{5,1},{2,6},{6,2},{3,7},{7,3},{8,12},{12,8},{9,1... | collective-permute-start | bytes 983048 | tf_op jit(solution)/shard_map/ppermute | solution.py:39
  247.6 21.2 %collective-permute-start.39 = (bf16[256,640]{1,0:T(8,128)(2,1)S(1)}, bf16[256,640]{1,0:T(8,128)(2,1)}, u32[]{:S(2)}, u32[]{:S(2)}) collective-permute-start(bf16[256,640]{1,0:T(8,128)(2,1)S(1)} %add_convert_fusion.5), channel_id=1, source_target_pairs={{0,1},{1,0},{2,3},{3,2},{4,5},{5,4},{6,7},{7,6},{8,9},{9,8},{10,11... | collective-permute-start | bytes 983048 | tf_op jit(solution)/shard_map/ppermute | solution.py:39
  277.0 31.5 %all-to-all-start.4 = ((bf16[4,160,640]{2,1,0:T(8,128)(2,1)}), bf16[4,160,640]{2,1,0:T(8,128)(2,1)}, u32[]{:S(2)}, u32[]{:S(2)}) async-start(bf16[4,160,640]{2,1,0:T(8,128)(2,1)} %bitcast.33), calls=%async_computation.4 | async-start | bytes 1638400 | tf_op jit(solution)/shard_map/all_to_all | solution.py:152
  297.6 14.1 %collective-permute-start.45 = (bf16[256,640]{1,0:T(8,128)(2,1)}, bf16[256,640]{1,0:T(8,128)(2,1)}, u32[]{:S(2)}, u32[]{:S(2)}) collective-permute-start(bf16[256,640]{1,0:T(8,128)(2,1)} %convolution_convert_fusion.8), channel_id=1, source_target_pairs={{0,4},{4,0},{1,5},{5,1},{2,6},{6,2},{3,7},{7,3},{8,12},{12,8},{9,1... | collective-permute-start | bytes 983048 | tf_op jit(solution)/shard_map/ppermute | solution.py:39
  312.9 49.0 %all-to-all-start.5 = ((bf16[4,640,640]{2,1,0:T(8,128)(2,1)}), bf16[4,640,640]{2,1,0:T(8,128)(2,1)S(1)}, u32[]{:S(2)}, u32[]{:S(2)}) async-start(bf16[4,640,640]{2,1,0:T(8,128)(2,1)} %pad_maximum_fusion.1), calls=%async_computation.5 | async-start | bytes 6553600 | tf_op jit(solution)/shard_map/all_to_all | solution.py:152
  321.6 12.0 %collective-permute-start.51 = (bf16[256,640]{1,0:T(8,128)(2,1)}, bf16[256,640]{1,0:T(8,128)(2,1)}, u32[]{:S(2)}, u32[]{:S(2)}) collective-permute-start(bf16[256,640]{1,0:T(8,128)(2,1)} %get-tuple-element.270.refs_4_), channel_id=1, source_target_pairs={{0,4},{4,0},{1,5},{5,1},{2,6},{6,2},{3,7},{7,3},{8,12},{12,8},{9,1... | collective-permute-start | bytes 983048 | tf_op jit(solution)/shard_map/ppermute | solution.py:39
  331.4 30.5 %collective-permute-start.50 = (bf16[480,640]{1,0:T(8,128)(2,1)S(1)}, bf16[480,640]{1,0:T(8,128)(2,1)}, u32[]{:S(2)}, u32[]{:S(2)}) collective-permute-start(bf16[480,640]{1,0:T(8,128)(2,1)S(1)} %pad_maximum_fusion.5), channel_id=1, source_target_pairs={{0,2},{2,0},{1,3},{3,1},{4,6},{6,4},{5,7},{7,5},{8,10},{10,8},{9,1... | collective-permute-start | bytes 1843208 | tf_op jit(solution)/shard_map/ppermute | solution.py:39
  363.1 12.1 %collective-permute-start.55 = (bf16[256,640]{1,0:T(8,128)(2,1)}, bf16[256,640]{1,0:T(8,128)(2,1)}, u32[]{:S(2)}, u32[]{:S(2)}) collective-permute-start(bf16[256,640]{1,0:T(8,128)(2,1)} %get-tuple-element.291), channel_id=1, source_target_pairs={{0,4},{4,0},{1,5},{5,1},{2,6},{6,2},{3,7},{7,3},{8,12},{12,8},{9,1... | collective-permute-start | bytes 983048 | tf_op jit(solution)/shard_map/ppermute | solution.py:39
  365.8 16.5 %collective-permute-start.56 = (bf16[256,640]{1,0:T(8,128)(2,1)}, bf16[256,640]{1,0:T(8,128)(2,1)}, u32[]{:S(2)}, u32[]{:S(2)}) collective-permute-start(bf16[256,640]{1,0:T(8,128)(2,1)} %add_convert_fusion.2), channel_id=1, source_target_pairs={{0,1},{1,0},{2,3},{3,2},{4,5},{5,4},{6,7},{7,6},{8,9},{9,8},{10,11... | collective-permute-start | bytes 983048 | tf_op jit(solution)/shard_map/ppermute | solution.py:39
  366.3 21.3 %collective-permute-start.57 = (bf16[320,640]{1,0:T(8,128)(2,1)S(1)}, bf16[320,640]{1,0:T(8,128)(2,1)S(1)}, u32[]{:S(2)}, u32[]{:S(2)}) collective-permute-start(bf16[320,640]{1,0:T(8,128)(2,1)S(1)} %slice.264), channel_id=1, source_target_pairs={{0,2},{2,0},{1,3},{3,1},{4,6},{6,4},{5,7},{7,5},{8,10},{10,8},{9,1... | collective-permute-start | bytes 1228808 | tf_op jit(solution)/shard_map/ppermute | solution.py:39
  371.2 20.5 %all-to-all-start.6 = ((bf16[4,160,640]{2,1,0:T(8,128)(2,1)}), bf16[4,160,640]{2,1,0:T(8,128)(2,1)S(1)}, u32[]{:S(2)}, u32[]{:S(2)}) async-start(bf16[4,160,640]{2,1,0:T(8,128)(2,1)} %bitcast.34), calls=%async_computation.6 | async-start | bytes 1638400 | tf_op jit(solution)/shard_map/all_to_all | solution.py:152
  393.1 23.5 %all-to-all-start.7 = ((bf16[4,320,640]{2,1,0:T(8,128)(2,1)}), bf16[4,320,640]{2,1,0:T(8,128)(2,1)S(1)}, u32[]{:S(2)}, u32[]{:S(2)}) async-start(bf16[4,320,640]{2,1,0:T(8,128)(2,1)} %broadcast_in_dim.70), calls=%async_computation.7 | async-start | bytes 3276800 | tf_op jit(solution)/shard_map/all_to_all | solution.py:152
  397.4 13.1 %collective-permute-start.59 = (bf16[192,640]{1,0:T(8,128)(2,1)S(1)}, bf16[192,640]{1,0:T(8,128)(2,1)S(1)}, u32[]{:S(2)}, u32[]{:S(2)}) collective-permute-start(bf16[192,640]{1,0:T(8,128)(2,1)S(1)} %pad_maximum_fusion.9), channel_id=1, source_target_pairs={{0,2},{2,0},{1,3},{3,1},{4,6},{6,4},{5,7},{7,5},{8,10},{10,8},{9,1... | collective-permute-start | bytes 737288 | tf_op jit(solution)/shard_map/ppermute | solution.py:39
  418.9 42.4 %all-to-all-start.8 = ((bf16[4,672,640]{2,1,0:T(8,128)(2,1)}), bf16[4,672,640]{2,1,0:T(8,128)(2,1)S(1)}, u32[]{:S(2)}, u32[]{:S(2)}) async-start(bf16[4,672,640]{2,1,0:T(8,128)(2,1)} %broadcast_in_dim.71), calls=%async_computation.8 | async-start | bytes 6881280 | tf_op jit(solution)/shard_map/all_to_all | solution.py:152
  422.7 11.9 %collective-permute-start.60 = (bf16[4,320,640]{2,1,0:T(8,128)(2,1)}, bf16[4,320,640]{2,1,0:T(8,128)(2,1)}, u32[]{:S(2)}, u32[]{:S(2)}) collective-permute-start(bf16[4,320,640]{2,1,0:T(8,128)(2,1)} %copy-done.10), channel_id=1, source_target_pairs={{0,4},{4,0},{1,5},{5,1},{2,6},{6,2},{3,7},{7,3},{8,12},{12,8},{9,1... | collective-permute-start | bytes 4915208 | tf_op jit(solution)/shard_map/ppermute | solution.py:39
  (110 other events, 978.2 us)

commit v2 on v1

--- a/solution.py
+++ b/solution.py
@@ -84,7 +84,7 @@
             jax.ShapeDtypeStruct((rows, model), BF),
         ],
         name="norm_forward",
-        **kernel_params(2.5),
+        **kernel_params(6),
     )(hidden, *parts, gain[None], bias[None])
 
 
@@ -588,7 +588,7 @@
         if first:
             far_0 = spread_rest(tie(far_0, sent), rest)
             attn_1 = flip(tie(far_attn(1), sent), "zh")
-            cotangent_home = rehome(tie(cotangent, attn_parts[2]))
+            cotangent_home = rehome(tie(cotangent, normed))
         else:
             far_1 = spread_rest(tie(far_1, sent), rest)
         middle, normed_two = norm_forward(

time: 492 us -> 481 us (0.978)
  waiting for transfers between devices: 133 us -> 126 us
    ppermute x58, waiting for transfers between devices: 103 us -> 87.3 us  [flip(): return lax.ppermute(x, axis, FLIP)]
    all_to_all x9, waiting for transfers between devices: 29.8 us -> 38.2 us  [exchange_rest(): return lax.all_to_all(x, 'r', 0, 0)]
    unnamed x141 -> x137, local copies, waits for them, and re-layouts: 12.4 us -> 12.5 us
  transfers between devices with their start and end apart: 73 -> 73, of which waited for: 30 -> 30; matrix products, arithmetic and copies ran while one was open for 21% -> 22% of each run, Pallas kernels for 22% -> 22%
where the time goes in v2:
time: 481 us; the launch traced here: 472 us
  waiting for transfers between devices  126 us (26%)
  Pallas kernels  111 us (23%)
  starting transfers between devices  105 us (22%)
  matrix products  56.7 us (12%)
  other arithmetic  35.9 us (7%)
  local copies, waits for them, and re-layouts  33 us (7%)
    ppermute x58, waiting for transfers between devices, flip(): return lax.ppermute(x, axis, FLIP)  87.3 us
    ppermute x58, starting transfers between devices, flip(): return lax.ppermute(x, axis, FLIP)  53.7 us
    pallas_call x2, Pallas kernels, attend_backward(): pl.pallas_call(kernel, grid=(4,), in_specs=[whole(rows, width3), pl.Block...  41.3 us
    all_to_all x9, waiting for transfers between devices, exchange_rest(): return lax.all_to_all(x, 'r', 0, 0)  38.2 us
    dot_general x23, matrix products, dot(): return jnp.dot(left, right, preferred_element_type=F32)  38.2 us
    all_to_all x9, starting transfers between devices, exchange_rest(): return lax.all_to_all(x, 'r', 0, 0)  36.2 us
    pallas_call x2, Pallas kernels, attend_forward(): pl.pallas_call(functools.partial(attend_forward_kernel, heads), grid=(2,)...  28 us
    dot_general x16, matrix products, dot_nt(): lax.dot_general(left, right, (((1,), (1,)), ((), ())), preferred_element_...  18.5 us
  transfers between devices with their start and end apart: 73, of which 30 were waited for; matrix products, arithmetic and copies ran while one was open for 22% of the time, Pallas kernels for 22%

profile of v2, /device:TPU:0, one launch (start us, length us, event | category | flops | bytes accessed | tf_op | source)
XLA Modules:
  0.0 472.2 jit_solution(4641563307799266648)
XLA Ops:
  18.9 7.0 %collective-permute-start.2 = (bf16[256,640]{1,0:T(8,128)(2,1)}, bf16[256,640]{1,0:T(8,128)(2,1)}, u32[]{:S(2)}, u32[]{:S(2)}) collective-permute-start(bf16[256,640]{1,0:T(8,128)(2,1)} %get-tuple-element.168.own_x_ref), channel_id=1, source_target_pairs={{0,4},{4,0},{1,5},{5,1},{2,6},{6,2},{3,7},{7,3},{8,12},{12,8},{9,1... | collective-permute-start | bytes 983048 | tf_op jit(solution)/shard_map/ppermute | solution.py:39
  25.9 8.9 %collective-permute-start.4 = (bf16[256,640]{1,0:T(8,128)(2,1)}, bf16[256,640]{1,0:T(8,128)(2,1)}, u32[]{:S(2)}, u32[]{:S(2)}) collective-permute-start(bf16[256,640]{1,0:T(8,128)(2,1)} %collective-permute-done.3.plane_x_ref), channel_id=1, source_target_pairs={{0,4},{4,0},{1,5},{5,1},{2,6},{6,2},{3,7},{7,3},{8,12},{12,8},{9,1... | collective-permute-start | bytes 983048 | tf_op jit(solution)/shard_map/ppermute | solution.py:39
  41.7 14.0 %attend_forward.2 = (bf16[256,640]{1,0:T(8,128)(2,1)}, bf16[256,640]{1,0:T(8,128)(2,1)}, bf16[256,640]{1,0:T(8,128)(2,1)}, bf16[256,640]{1,0:T(8,128)(2,1)}, bf1...) custom-call(bf16[256,640]{1,0:T(8,128)(2,1)} %get-tuple-element.168.own_x_ref, ...), custom_call_target="tpu_custom_call" | custom-call | flops 4600000000 | bytes 1048576 | tf_op jit(solution)/shard_map/attend_forward/pallas_call | solution.py:326
  55.7 4.2 collective-permute-done.7
  68.6 4.0 collective-permute-done.10.refs_2_
  77.5 4.1 collective-permute-start.16
  83.7 3.9 collective-permute-done.12
  89.9 4.4 ffn_weights_here.2
  120.3 5.9 %all-to-all-done.1 = bf16[4,160,640]{2,1,0:T(8,128)(2,1)S(1)} async-done(((bf16[4,160,640]{2,1,0:T(8,128)(2,1)}), bf16[4,160,640]{2,1,0:T(8,128)(2,1)S(1)}, u32[]{:S(2)}, u32[]{:S(2)}) %all-to-all-start.1) | async-done | bytes 819232 | tf_op jit(solution)/shard_map/all_to_all | solution.py:152
  132.2 14.1 %attend_forward.3 = (bf16[256,640]{1,0:T(8,128)(2,1)}, bf16[256,640]{1,0:T(8,128)(2,1)}, bf16[256,640]{1,0:T(8,128)(2,1)}, bf16[256,640]{1,0:T(8,128)(2,1)}, bf1...) custom-call(bf16[256,640]{1,0:T(8,128)(2,1)} %get-tuple-element.199.own_x_ref, ...), custom_call_target="tpu_custom_call" | custom-call | flops 4600000000 | bytes 1048576 | tf_op jit(solution)/shard_map/attend_forward/pallas_call | solution.py:326
  146.2 4.3 collective-permute-done.22
  159.7 4.8 %collective-permute-done.25.refs_2_ = bf16[256,640]{1,0:T(8,128)(2,1)} collective-permute-done((bf16[256,640]{1,0:T(8,128)(2,1)}, bf16[256,640]{1,0:T(8,128)(2,1)}, u32[]{:S(2)}, u32[]{:S(2)}) %collective-permute-start.25) | collective-permute-done | bytes 327712 | tf_op jit(solution)/shard_map/ppermute | solution.py:39
  167.3 9.0 %collective-permute-done.27 = bf16[256,640]{1,0:T(8,128)(2,1)} collective-permute-done((bf16[256,640]{1,0:T(8,128)(2,1)}, bf16[256,640]{1,0:T(8,128)(2,1)}, u32[]{:S(2)}, u32[]{:S(2)}) %collective-permute-start.27) | collective-permute-done | bytes 327712 | tf_op jit(solution)/shard_map/ppermute | solution.py:39
  181.1 4.8 %ffn_weights_here.3 = (bf16[640,1280]{1,0:T(8,128)(2,1)}, bf16[2,640,640]{2,1,0:T(8,128)(2,1)}) custom-call(s32[1]{0:T(128)} %bitcast.11.place_ref, bf16[2,640,1280]{2,1,0:T(8,128)(2,1)} %up_home_ref.3, bf16[2,2,640,640]{3,2,1,0:T(8,128)(2,1)} %bitcast.159, bf16[4,320,640]{2,1,0:T(8,128)(2,1)} %copy-done.12), custom_call_target="tpu_custom_call" | custom-call | flops 4600000000 | bytes 1048576 | tf_op jit(solution)/shard_map/ffn_weights_here/pallas_call | solution.py:181
  214.8 4.8 %all-to-all-start.3 = ((bf16[4,640,640]{2,1,0:T(8,128)(2,1)}), bf16[4,640,640]{2,1,0:T(8,128)(2,1)}, u32[]{:S(2)}, u32[]{:S(2)}) async-start(bf16[4,640,640]{2,1,0:T(8,128)(2,1)} %pad_maximum_fusion), calls=%async_computation.3 | async-start | bytes 6553600 | tf_op jit(solution)/shard_map/all_to_all | solution.py:152
  227.5 5.8 %collective-permute-done.36.refs_6_ = bf16[256,640]{1,0:T(8,128)(2,1)S(1)} collective-permute-done((bf16[256,640]{1,0:T(8,128)(2,1)}, bf16[256,640]{1,0:T(8,128)(2,1)S(1)}, u32[]{:S(2)}, u32[]{:S(2)}) %collective-permute-start.36) | collective-permute-done | bytes 327712 | tf_op jit(solution)/shard_map/ppermute | solution.py:39
  238.2 20.6 %attend_backward.2 = (bf16[256,640]{1,0:T(8,128)(2,1)}, bf16[256,640]{1,0:T(8,128)(2,1)}, bf16[256,640]{1,0:T(8,128)(2,1)}, bf16[256,640]{1,0:T(8,128)(2,1)}, bf...) custom-call(bf16[1024,480]{1,0:T(8,128)(2,1)} %get-tuple-element.233.refs_0_, f32[1024,1024]{1,0:T(8,128)} %fusion.1.bias_ref.refs_1_, ...), custom_call_target="tpu_custom_call" | custom-call | flops 6899999744 | bytes 1048576 | tf_op jit(solution)/shard_map/attend_backward/pallas_call | solution.py:454
  266.0 4.4 all-to-all-start.4
  279.4 5.4 %collective-permute-done.46 = bf16[256,640]{1,0:T(8,128)(2,1)S(1)} collective-permute-done((bf16[256,640]{1,0:T(8,128)(2,1)}, bf16[256,640]{1,0:T(8,128)(2,1)S(1)}, u32[]{:S(2)}, u32[]{:S(2)}) %collective-permute-start.46) | collective-permute-done | bytes 327712 | tf_op jit(solution)/shard_map/ppermute | solution.py:39
  302.4 4.1 all-to-all-start.5
  314.1 4.6 collective-permute-done.52.refs_6_
  324.0 20.6 %attend_backward.3 = (bf16[256,640]{1,0:T(8,128)(2,1)}, bf16[256,640]{1,0:T(8,128)(2,1)}, bf16[256,640]{1,0:T(8,128)(2,1)}, bf16[256,640]{1,0:T(8,128)(2,1)}, bf...) custom-call(bf16[1024,480]{1,0:T(8,128)(2,1)} %get-tuple-element.273.refs_0_, f32[1024,1024]{1,0:T(8,128)} %fusion.1.bias_ref.refs_1_, ...), custom_call_target="tpu_custom_call" | custom-call | flops 6899999744 | bytes 1048576 | tf_op jit(solution)/shard_map/attend_backward/pallas_call | solution.py:454
  344.6 6.6 %collective-permute-done.50 = bf16[480,640]{1,0:T(8,128)(2,1)} collective-permute-done((bf16[480,640]{1,0:T(8,128)(2,1)S(1)}, bf16[480,640]{1,0:T(8,128)(2,1)}, u32[]{:S(2)}, u32[]{:S(2)}) %collective-permute-start.50) | collective-permute-done | bytes 614432 | tf_op jit(solution)/shard_map/ppermute | solution.py:39
  365.1 6.5 %collective-permute-done.56.plane_ref = bf16[256,640]{1,0:T(8,128)(2,1)} collective-permute-done((bf16[256,640]{1,0:T(8,128)(2,1)}, bf16[256,640]{1,0:T(8,128)(2,1)}, u32[]{:S(2)}, u32[]{:S(2)}) %collective-permute-start.56) | collective-permute-done | bytes 327712 | tf_op jit(solution)/shard_map/ppermute | solution.py:39
  371.6 6.0 %collective-permute-done.57 = bf16[320,640]{1,0:T(8,128)(2,1)S(1)} collective-permute-done((bf16[320,640]{1,0:T(8,128)(2,1)S(1)}, bf16[320,640]{1,0:T(8,128)(2,1)S(1)}, u32[]{:S(2)}, u32[]{:S(2)}) %collective-permute-start.57) | collective-permute-done | bytes 409632 | tf_op jit(solution)/shard_map/ppermute | solution.py:39
  383.0 4.0 all-to-all-start.7
  391.5 8.9 %collective-permute-done.59 = bf16[192,640]{1,0:T(8,128)(2,1)S(1)} collective-permute-done((bf16[192,640]{1,0:T(8,128)(2,1)S(1)}, bf16[192,640]{1,0:T(8,128)(2,1)S(1)}, u32[]{:S(2)}, u32[]{:S(2)}) %collective-permute-start.59) | collective-permute-done | bytes 245792 | tf_op jit(solution)/shard_map/ppermute | solution.py:39
  400.7 5.8 %all-to-all-done.7.mine_ref = bf16[4,320,640]{2,1,0:T(8,128)(2,1)S(1)} async-done(((bf16[4,320,640]{2,1,0:T(8,128)(2,1)}), bf16[4,320,640]{2,1,0:T(8,128)(2,1)S(1)}, u32[]{:S(2)}, u32[]{:S(2)}) %all-to-all-start.7) | async-done | bytes 1638432 | tf_op jit(solution)/shard_map/all_to_all | solution.py:152
  424.5 5.1 %ffn_grads.2 = (f32[2,640,1280]{2,1,0:T(8,128)}, f32[2,2,640,640]{3,2,1,0:T(8,128)}) custom-call(s32[1]{0:T(128)} %bitcast.11.place_ref, bf16[4,320,640]{2,1,0:T(8,128)(2,1)} %copy-done.10, bf16[4,320,640]{2,1,0:T(8,128)(2,1)} %collective-permute-done.60.other_ref), custom_call_target="tpu_custom_call" | custom-call | flops 4600000000 | bytes 1048576 | tf_op jit(solution)/shard_map/ffn_grads/pallas_call | solution.py:225
  429.6 21.7 %all-to-all-done.8.mine_ref = bf16[4,672,640]{2,1,0:T(8,128)(2,1)S(1)} async-done(((bf16[4,672,640]{2,1,0:T(8,128)(2,1)}), bf16[4,672,640]{2,1,0:T(8,128)(2,1)S(1)}, u32[]{:S(2)}, u32[]{:S(2)}) %all-to-all-start.8) | async-done | bytes 3440672 | tf_op jit(solution)/shard_map/all_to_all | solution.py:152
  453.4 4.0 collective-permute-done.63.other_ref
  463.8 5.1 %ffn_grads.3 = (f32[2,640,1280]{2,1,0:T(8,128)}, f32[2,2,640,640]{3,2,1,0:T(8,128)}) custom-call(s32[1]{0:T(128)} %bitcast.11.place_ref, bf16[4,672,640]{2,1,0:T(8,128)(2,1)} %copy-done.3, bf16[4,672,640]{2,1,0:T(8,128)(2,1)} %copy-done.4, f32[2,640,1280]{2,1,0:T(8,128)} %get-tuple-element.313.refs_0_, ...), custom_call_target="tpu_custom_call", output_to_operand_aliasing={{0}: (3, {}), {1}: (4, {})} | custom-call | flops 4600000000 | bytes 1048576 | tf_op jit(solution)/shard_map/ffn_grads/pallas_call | solution.py:225
  (390 shorter events, 230.1 us)
Async XLA Ops:
  5.2 35.8 %collective-permute-start.6 = (bf16[160,640]{1,0:T(8,128)(2,1)S(1)}, bf16[160,640]{1,0:T(8,128)(2,1)S(1)}, u32[]{:S(2)}, u32[]{:S(2)}) collective-permute-start(bf16[160,640]{1,0:T(8,128)(2,1)S(1)} %get-tuple-element.339), channel_id=1, source_target_pairs={{0,0},{1,1},{2,4},{3,5},{4,2},{5,3},{6,6},{7,7},{8,8},{9,9},{10,12... | collective-permute-start | bytes 614408 | tf_op jit(solution)/shard_map/ppermute | solution.py:35
  7.3 33.7 %collective-permute-start.5 = (bf16[480,640]{1,0:T(8,128)(2,1)S(1)}, bf16[480,640]{1,0:T(8,128)(2,1)}, u32[]{:S(2)}, u32[]{:S(2)}) collective-permute-start(bf16[480,640]{1,0:T(8,128)(2,1)S(1)} %bitcast.161), channel_id=1, source_target_pairs={{0,0},{1,1},{2,4},{3,5},{4,2},{5,3},{6,6},{7,7},{8,8},{9,9},{10,12... | collective-permute-start | bytes 1843208 | tf_op jit(solution)/shard_map/ppermute | solution.py:35
  18.9 22.1 %collective-permute-start.2 = (bf16[256,640]{1,0:T(8,128)(2,1)}, bf16[256,640]{1,0:T(8,128)(2,1)}, u32[]{:S(2)}, u32[]{:S(2)}) collective-permute-start(bf16[256,640]{1,0:T(8,128)(2,1)} %get-tuple-element.168.own_x_ref), channel_id=1, source_target_pairs={{0,4},{4,0},{1,5},{5,1},{2,6},{6,2},{3,7},{7,3},{8,12},{12,8},{9,1... | collective-permute-start | bytes 983048 | tf_op jit(solution)/shard_map/ppermute | solution.py:39
  25.9 15.1 %collective-permute-start.4 = (bf16[256,640]{1,0:T(8,128)(2,1)}, bf16[256,640]{1,0:T(8,128)(2,1)}, u32[]{:S(2)}, u32[]{:S(2)}) collective-permute-start(bf16[256,640]{1,0:T(8,128)(2,1)} %collective-permute-done.3.plane_x_ref), channel_id=1, source_target_pairs={{0,4},{4,0},{1,5},{5,1},{2,6},{6,2},{3,7},{7,3},{8,12},{12,8},{9,1... | collective-permute-start | bytes 983048 | tf_op jit(solution)/shard_map/ppermute | solution.py:39
  37.8 22.1 %collective-permute-start.7 = (bf16[320,640]{1,0:T(8,128)(2,1)S(1)}, bf16[320,640]{1,0:T(8,128)(2,1)S(1)}, u32[]{:S(2)}, u32[]{:S(2)}) collective-permute-start(bf16[320,640]{1,0:T(8,128)(2,1)S(1)} %pad_maximum_fusion.7), channel_id=1, source_target_pairs={{0,2},{2,0},{1,3},{3,1},{4,6},{6,4},{5,7},{7,5},{8,10},{10,8},{9,1... | collective-permute-start | bytes 1228808 | tf_op jit(solution)/shard_map/ppermute | solution.py:39
  64.9 23.8 %all-to-all-start = ((bf16[4,320,640]{2,1,0:T(8,128)(2,1)}), bf16[4,320,640]{2,1,0:T(8,128)(2,1)S(1)}, u32[]{:S(2)}, u32[]{:S(2)}) async-start(bf16[4,320,640]{2,1,0:T(8,128)(2,1)} %broadcast_in_dim.32), calls=%async_computation | async-start | bytes 3276800 | tf_op jit(solution)/shard_map/all_to_all | solution.py:152
  77.5 23.5 %collective-permute-start.16 = (bf16[256,640]{1,0:T(8,128)(2,1)}, bf16[256,640]{1,0:T(8,128)(2,1)}, u32[]{:S(2)}, u32[]{:S(2)}) collective-permute-start(bf16[256,640]{1,0:T(8,128)(2,1)} %param.23), channel_id=1, source_target_pairs={{0,0},{1,1},{2,4},{3,5},{4,2},{5,3},{6,6},{7,7},{8,8},{9,9},{10,12... | collective-permute-start | bytes 983048 | tf_op jit(solution)/shard_map/ppermute | solution.py:35
  81.5 19.4 %collective-permute-start.15 = (bf16[160,640]{1,0:T(8,128)(2,1)}, bf16[160,640]{1,0:T(8,128)(2,1)S(1)}, u32[]{:S(2)}, u32[]{:S(2)}) collective-permute-start(bf16[160,640]{1,0:T(8,128)(2,1)} %fusion.101), channel_id=1, source_target_pairs={{0,2},{2,0},{1,3},{3,1},{4,6},{6,4},{5,7},{7,5},{8,10},{10,8},{9,1... | collective-permute-start | bytes 614408 | tf_op jit(solution)/shard_map/ppermute | solution.py:39
  111.1 15.1 %all-to-all-start.1 = ((bf16[4,160,640]{2,1,0:T(8,128)(2,1)}), bf16[4,160,640]{2,1,0:T(8,128)(2,1)S(1)}, u32[]{:S(2)}, u32[]{:S(2)}) async-start(bf16[4,160,640]{2,1,0:T(8,128)(2,1)} %broadcast_in_dim.33), calls=%async_computation.1 | async-start | bytes 1638400 | tf_op jit(solution)/shard_map/all_to_all | solution.py:152
  128.9 21.6 %collective-permute-start.22 = (bf16[320,640]{1,0:T(8,128)(2,1)S(1)}, bf16[320,640]{1,0:T(8,128)(2,1)S(1)}, u32[]{:S(2)}, u32[]{:S(2)}) collective-permute-start(bf16[320,640]{1,0:T(8,128)(2,1)S(1)} %copy-done.30), channel_id=1, source_target_pairs={{0,2},{2,0},{1,3},{3,1},{4,6},{6,4},{5,7},{7,5},{8,10},{10,8},{9,1... | collective-permute-start | bytes 1228808 | tf_op jit(solution)/shard_map/ppermute | solution.py:39
  156.0 24.0 %all-to-all-start.2 = ((bf16[4,320,640]{2,1,0:T(8,128)(2,1)}), bf16[4,320,640]{2,1,0:T(8,128)(2,1)S(1)}, u32[]{:S(2)}, u32[]{:S(2)}) async-start(bf16[4,320,640]{2,1,0:T(8,128)(2,1)} %broadcast_in_dim.34), calls=%async_computation.2 | async-start | bytes 3276800 | tf_op jit(solution)/shard_map/all_to_all | solution.py:152
  167.3 18.6 %collective-permute-start.26 = (bf16[256,640]{1,0:T(8,128)(2,1)}, bf16[256,640]{1,0:T(8,128)(2,1)}, u32[]{:S(2)}, u32[]{:S(2)}) collective-permute-start(bf16[256,640]{1,0:T(8,128)(2,1)} %get-tuple-element.225), channel_id=1, source_target_pairs={{0,4},{4,0},{1,5},{5,1},{2,6},{6,2},{3,7},{7,3},{8,12},{12,8},{9,1... | collective-permute-start | bytes 983048 | tf_op jit(solution)/shard_map/ppermute | solution.py:39
  186.0 12.5 %collective-permute-start.32 = (bf16[256,640]{1,0:T(8,128)(2,1)}, bf16[256,640]{1,0:T(8,128)(2,1)S(1)}, u32[]{:S(2)}, u32[]{:S(2)}) collective-permute-start(bf16[256,640]{1,0:T(8,128)(2,1)} %collective-permute-done.16.grad_ref), channel_id=1, source_target_pairs={{0,4},{4,0},{1,5},{5,1},{2,6},{6,2},{3,7},{7,3},{8,12},{12,8},{9,1... | collective-permute-start | bytes 983048 | tf_op jit(solution)/shard_map/ppermute | solution.py:39
  186.0 12.2 %collective-permute-start.29 = (bf16[256,640]{1,0:T(8,128)(2,1)}, bf16[256,640]{1,0:T(8,128)(2,1)S(1)}, u32[]{:S(2)}, u32[]{:S(2)}) collective-permute-start(bf16[256,640]{1,0:T(8,128)(2,1)} %collective-permute-done.16.grad_ref), channel_id=1, source_target_pairs={{0,1},{1,0},{2,3},{3,2},{4,5},{5,4},{6,7},{7,6},{8,9},{9,8},{10,11... | collective-permute-start | bytes 983048 | tf_op jit(solution)/shard_map/ppermute | solution.py:39
  200.7 19.0 %collective-permute-start.33 = (bf16[256,640]{1,0:T(8,128)(2,1)}, bf16[256,640]{1,0:T(8,128)(2,1)S(1)}, u32[]{:S(2)}, u32[]{:S(2)}) collective-permute-start(bf16[256,640]{1,0:T(8,128)(2,1)} %convolution_convert_fusion.14), channel_id=1, source_target_pairs={{0,4},{4,0},{1,5},{5,1},{2,6},{6,2},{3,7},{7,3},{8,12},{12,8},{9,1... | collective-permute-start | bytes 983048 | tf_op jit(solution)/shard_map/ppermute | solution.py:39
  205.8 14.0 %collective-permute-start.34 = (bf16[256,640]{1,0:T(8,128)(2,1)}, bf16[256,640]{1,0:T(8,128)(2,1)}, u32[]{:S(2)}, u32[]{:S(2)}) collective-permute-start(bf16[256,640]{1,0:T(8,128)(2,1)} %add_convert_fusion.6), channel_id=1, source_target_pairs={{0,1},{1,0},{2,3},{3,2},{4,5},{5,4},{6,7},{7,6},{8,9},{9,8},{10,11... | collective-permute-start | bytes 983048 | tf_op jit(solution)/shard_map/ppermute | solution.py:39
  214.8 44.1 %all-to-all-start.3 = ((bf16[4,640,640]{2,1,0:T(8,128)(2,1)}), bf16[4,640,640]{2,1,0:T(8,128)(2,1)}, u32[]{:S(2)}, u32[]{:S(2)}) async-start(bf16[4,640,640]{2,1,0:T(8,128)(2,1)} %pad_maximum_fusion), calls=%async_computation.3 | async-start | bytes 6553600 | tf_op jit(solution)/shard_map/all_to_all | solution.py:152
  235.3 23.6 %collective-permute-start.40 = (bf16[256,640]{1,0:T(8,128)(2,1)S(1)}, bf16[256,640]{1,0:T(8,128)(2,1)}, u32[]{:S(2)}, u32[]{:S(2)}) collective-permute-start(bf16[256,640]{1,0:T(8,128)(2,1)S(1)} %convolution_convert_fusion.12), channel_id=1, source_target_pairs={{0,4},{4,0},{1,5},{5,1},{2,6},{6,2},{3,7},{7,3},{8,12},{12,8},{9,1... | collective-permute-start | bytes 983048 | tf_op jit(solution)/shard_map/ppermute | solution.py:39
  236.6 22.3 %collective-permute-start.39 = (bf16[256,640]{1,0:T(8,128)(2,1)S(1)}, bf16[256,640]{1,0:T(8,128)(2,1)}, u32[]{:S(2)}, u32[]{:S(2)}) collective-permute-start(bf16[256,640]{1,0:T(8,128)(2,1)S(1)} %add_convert_fusion.5), channel_id=1, source_target_pairs={{0,1},{1,0},{2,3},{3,2},{4,5},{5,4},{6,7},{7,6},{8,9},{9,8},{10,11... | collective-permute-start | bytes 983048 | tf_op jit(solution)/shard_map/ppermute | solution.py:39
  266.0 31.9 %all-to-all-start.4 = ((bf16[4,160,640]{2,1,0:T(8,128)(2,1)}), bf16[4,160,640]{2,1,0:T(8,128)(2,1)}, u32[]{:S(2)}, u32[]{:S(2)}) async-start(bf16[4,160,640]{2,1,0:T(8,128)(2,1)} %bitcast.33), calls=%async_computation.4 | async-start | bytes 1638400 | tf_op jit(solution)/shard_map/all_to_all | solution.py:152
  287.1 13.9 %collective-permute-start.45 = (bf16[256,640]{1,0:T(8,128)(2,1)}, bf16[256,640]{1,0:T(8,128)(2,1)}, u32[]{:S(2)}, u32[]{:S(2)}) collective-permute-start(bf16[256,640]{1,0:T(8,128)(2,1)} %convolution_convert_fusion.8), channel_id=1, source_target_pairs={{0,4},{4,0},{1,5},{5,1},{2,6},{6,2},{3,7},{7,3},{8,12},{12,8},{9,1... | collective-permute-start | bytes 983048 | tf_op jit(solution)/shard_map/ppermute | solution.py:39
  302.4 48.9 %all-to-all-start.5 = ((bf16[4,640,640]{2,1,0:T(8,128)(2,1)}), bf16[4,640,640]{2,1,0:T(8,128)(2,1)S(1)}, u32[]{:S(2)}, u32[]{:S(2)}) async-start(bf16[4,640,640]{2,1,0:T(8,128)(2,1)} %pad_maximum_fusion.1), calls=%async_computation.5 | async-start | bytes 6553600 | tf_op jit(solution)/shard_map/all_to_all | solution.py:152
  310.6 12.7 %collective-permute-start.51 = (bf16[256,640]{1,0:T(8,128)(2,1)}, bf16[256,640]{1,0:T(8,128)(2,1)}, u32[]{:S(2)}, u32[]{:S(2)}) collective-permute-start(bf16[256,640]{1,0:T(8,128)(2,1)} %get-tuple-element.270.refs_4_), channel_id=1, source_target_pairs={{0,4},{4,0},{1,5},{5,1},{2,6},{6,2},{3,7},{7,3},{8,12},{12,8},{9,1... | collective-permute-start | bytes 983048 | tf_op jit(solution)/shard_map/ppermute | solution.py:39
  320.8 30.5 %collective-permute-start.50 = (bf16[480,640]{1,0:T(8,128)(2,1)S(1)}, bf16[480,640]{1,0:T(8,128)(2,1)}, u32[]{:S(2)}, u32[]{:S(2)}) collective-permute-start(bf16[480,640]{1,0:T(8,128)(2,1)S(1)} %pad_maximum_fusion.5), channel_id=1, source_target_pairs={{0,2},{2,0},{1,3},{3,1},{4,6},{6,4},{5,7},{7,5},{8,10},{10,8},{9,1... | collective-permute-start | bytes 1843208 | tf_op jit(solution)/shard_map/ppermute | solution.py:39
  352.4 12.6 %collective-permute-start.55 = (bf16[256,640]{1,0:T(8,128)(2,1)}, bf16[256,640]{1,0:T(8,128)(2,1)}, u32[]{:S(2)}, u32[]{:S(2)}) collective-permute-start(bf16[256,640]{1,0:T(8,128)(2,1)} %get-tuple-element.291), channel_id=1, source_target_pairs={{0,4},{4,0},{1,5},{5,1},{2,6},{6,2},{3,7},{7,3},{8,12},{12,8},{9,1... | collective-permute-start | bytes 983048 | tf_op jit(solution)/shard_map/ppermute | solution.py:39
  355.1 16.5 %collective-permute-start.56 = (bf16[256,640]{1,0:T(8,128)(2,1)}, bf16[256,640]{1,0:T(8,128)(2,1)}, u32[]{:S(2)}, u32[]{:S(2)}) collective-permute-start(bf16[256,640]{1,0:T(8,128)(2,1)} %add_convert_fusion.2), channel_id=1, source_target_pairs={{0,1},{1,0},{2,3},{3,2},{4,5},{5,4},{6,7},{7,6},{8,9},{9,8},{10,11... | collective-permute-start | bytes 983048 | tf_op jit(solution)/shard_map/ppermute | solution.py:39
  355.7 21.9 %collective-permute-start.57 = (bf16[320,640]{1,0:T(8,128)(2,1)S(1)}, bf16[320,640]{1,0:T(8,128)(2,1)S(1)}, u32[]{:S(2)}, u32[]{:S(2)}) collective-permute-start(bf16[320,640]{1,0:T(8,128)(2,1)S(1)} %slice.264), channel_id=1, source_target_pairs={{0,2},{2,0},{1,3},{3,1},{4,6},{6,4},{5,7},{7,5},{8,10},{10,8},{9,1... | collective-permute-start | bytes 1228808 | tf_op jit(solution)/shard_map/ppermute | solution.py:39
  361.2 20.5 %all-to-all-start.6 = ((bf16[4,160,640]{2,1,0:T(8,128)(2,1)}), bf16[4,160,640]{2,1,0:T(8,128)(2,1)S(1)}, u32[]{:S(2)}, u32[]{:S(2)}) async-start(bf16[4,160,640]{2,1,0:T(8,128)(2,1)} %bitcast.34), calls=%async_computation.6 | async-start | bytes 1638400 | tf_op jit(solution)/shard_map/all_to_all | solution.py:152
  383.0 23.4 %all-to-all-start.7 = ((bf16[4,320,640]{2,1,0:T(8,128)(2,1)}), bf16[4,320,640]{2,1,0:T(8,128)(2,1)S(1)}, u32[]{:S(2)}, u32[]{:S(2)}) async-start(bf16[4,320,640]{2,1,0:T(8,128)(2,1)} %broadcast_in_dim.70), calls=%async_computation.7 | async-start | bytes 3276800 | tf_op jit(solution)/shard_map/all_to_all | solution.py:152
  387.3 13.1 %collective-permute-start.59 = (bf16[192,640]{1,0:T(8,128)(2,1)S(1)}, bf16[192,640]{1,0:T(8,128)(2,1)S(1)}, u32[]{:S(2)}, u32[]{:S(2)}) collective-permute-start(bf16[192,640]{1,0:T(8,128)(2,1)S(1)} %pad_maximum_fusion.9), channel_id=1, source_target_pairs={{0,2},{2,0},{1,3},{3,1},{4,6},{6,4},{5,7},{7,5},{8,10},{10,8},{9,1... | collective-permute-start | bytes 737288 | tf_op jit(solution)/shard_map/ppermute | solution.py:39
  408.8 42.4 %all-to-all-start.8 = ((bf16[4,672,640]{2,1,0:T(8,128)(2,1)}), bf16[4,672,640]{2,1,0:T(8,128)(2,1)S(1)}, u32[]{:S(2)}, u32[]{:S(2)}) async-start(bf16[4,672,640]{2,1,0:T(8,128)(2,1)} %broadcast_in_dim.71), calls=%async_computation.8 | async-start | bytes 6881280 | tf_op jit(solution)/shard_map/all_to_all | solution.py:152
  412.6 11.9 %collective-permute-start.60 = (bf16[4,320,640]{2,1,0:T(8,128)(2,1)}, bf16[4,320,640]{2,1,0:T(8,128)(2,1)}, u32[]{:S(2)}, u32[]{:S(2)}) collective-permute-start(bf16[4,320,640]{2,1,0:T(8,128)(2,1)} %copy-done.10), channel_id=1, source_target_pairs={{0,4},{4,0},{1,5},{5,1},{2,6},{6,2},{3,7},{7,3},{8,12},{12,8},{9,1... | collective-permute-start | bytes 4915208 | tf_op jit(solution)/shard_map/ppermute | solution.py:39
  (108 other events, 974.3 us)

commit v3 on v2

--- a/solution.py
+++ b/solution.py
@@ -586,11 +586,11 @@
         sent, came = scatter_far(*attn_parts[2:])
         attn_parts = (attn_parts[0], flip(attn_parts[1], "c"), came)
         if first:
-            far_0 = spread_rest(tie(far_0, sent), rest)
+            far_0 = spread_rest(tie(far_0, attn_parts[1]), rest)
             attn_1 = flip(tie(far_attn(1), sent), "zh")
             cotangent_home = rehome(tie(cotangent, normed))
         else:
-            far_1 = spread_rest(tie(far_1, sent), rest)
+            far_1 = spread_rest(tie(far_1, attn_parts[1]), rest)
         middle, normed_two = norm_forward(
             hidden, attn_parts, ln_gain[depth, 1], ln_bias[depth, 1]
         )

time: 481 us -> 481 us (level)
  no operation moved by 1% of the time
where the time goes in v3:
time: 481 us; the launch traced here: 472 us
  waiting for transfers between devices  126 us (26%)
  Pallas kernels  111 us (23%)
  starting transfers between devices  105 us (22%)
  matrix products  56.8 us (12%)
  other arithmetic  35.9 us (7%)
  local copies, waits for them, and re-layouts  33 us (7%)
    ppermute x58, waiting for transfers between devices, flip(): return lax.ppermute(x, axis, FLIP)  87.5 us
    ppermute x58, starting transfers between devices, flip(): return lax.ppermute(x, axis, FLIP)  53.5 us
    pallas_call x2, Pallas kernels, attend_backward(): pl.pallas_call(kernel, grid=(4,), in_specs=[whole(rows, width3), pl.Block...  41.3 us
    all_to_all x9, waiting for transfers between devices, exchange_rest(): return lax.all_to_all(x, 'r', 0, 0)  38.2 us
    dot_general x23, matrix products, dot(): return jnp.dot(left, right, preferred_element_type=F32)  38.2 us
    all_to_all x9, starting transfers between devices, exchange_rest(): return lax.all_to_all(x, 'r', 0, 0)  36.2 us
    pallas_call x2, Pallas kernels, attend_forward(): pl.pallas_call(functools.partial(attend_forward_kernel, heads), grid=(2,)...  28 us
    dot_general x16, matrix products, dot_nt(): lax.dot_general(left, right, (((1,), (1,)), ((), ())), preferred_element_...  18.6 us
  transfers between devices with their start and end apart: 73, of which 30 were waited for; matrix products, arithmetic and copies ran while one was open for 22% of the time, Pallas kernels for 22%

profile of v3, /device:TPU:0, one launch (start us, length us, event | category | flops | bytes accessed | tf_op | source)
XLA Modules:
  0.0 472.1 jit_solution(996687436818759841)
XLA Ops:
  18.9 7.0 %collective-permute-start.2 = (bf16[256,640]{1,0:T(8,128)(2,1)}, bf16[256,640]{1,0:T(8,128)(2,1)}, u32[]{:S(2)}, u32[]{:S(2)}) collective-permute-start(bf16[256,640]{1,0:T(8,128)(2,1)} %get-tuple-element.168.own_x_ref), channel_id=1, source_target_pairs={{0,4},{4,0},{1,5},{5,1},{2,6},{6,2},{3,7},{7,3},{8,12},{12,8},{9,1... | collective-permute-start | bytes 983048 | tf_op jit(solution)/shard_map/ppermute | solution.py:39
  25.9 8.9 %collective-permute-start.4 = (bf16[256,640]{1,0:T(8,128)(2,1)}, bf16[256,640]{1,0:T(8,128)(2,1)}, u32[]{:S(2)}, u32[]{:S(2)}) collective-permute-start(bf16[256,640]{1,0:T(8,128)(2,1)} %collective-permute-done.3.plane_x_ref), channel_id=1, source_target_pairs={{0,4},{4,0},{1,5},{5,1},{2,6},{6,2},{3,7},{7,3},{8,12},{12,8},{9,1... | collective-permute-start | bytes 983048 | tf_op jit(solution)/shard_map/ppermute | solution.py:39
  41.7 14.0 %attend_forward.2 = (bf16[256,640]{1,0:T(8,128)(2,1)}, bf16[256,640]{1,0:T(8,128)(2,1)}, bf16[256,640]{1,0:T(8,128)(2,1)}, bf16[256,640]{1,0:T(8,128)(2,1)}, bf1...) custom-call(bf16[256,640]{1,0:T(8,128)(2,1)} %get-tuple-element.168.own_x_ref, ...), custom_call_target="tpu_custom_call" | custom-call | flops 4600000000 | bytes 1048576 | tf_op jit(solution)/shard_map/attend_forward/pallas_call | solution.py:326
  55.7 4.2 collective-permute-done.7
  68.6 4.0 collective-permute-done.10.refs_2_
  77.5 4.1 collective-permute-start.16
  83.7 3.9 collective-permute-done.12
  89.9 4.4 ffn_weights_here.2
  120.3 5.9 %all-to-all-done.1 = bf16[4,160,640]{2,1,0:T(8,128)(2,1)S(1)} async-done(((bf16[4,160,640]{2,1,0:T(8,128)(2,1)}), bf16[4,160,640]{2,1,0:T(8,128)(2,1)S(1)}, u32[]{:S(2)}, u32[]{:S(2)}) %all-to-all-start.1) | async-done | bytes 819232 | tf_op jit(solution)/shard_map/all_to_all | solution.py:152
  132.2 14.0 %attend_forward.3 = (bf16[256,640]{1,0:T(8,128)(2,1)}, bf16[256,640]{1,0:T(8,128)(2,1)}, bf16[256,640]{1,0:T(8,128)(2,1)}, bf16[256,640]{1,0:T(8,128)(2,1)}, bf1...) custom-call(bf16[256,640]{1,0:T(8,128)(2,1)} %get-tuple-element.199.own_x_ref, ...), custom_call_target="tpu_custom_call" | custom-call | flops 4600000000 | bytes 1048576 | tf_op jit(solution)/shard_map/attend_forward/pallas_call | solution.py:326
  146.2 4.2 collective-permute-done.22
  159.8 4.8 %collective-permute-done.25.refs_2_ = bf16[256,640]{1,0:T(8,128)(2,1)} collective-permute-done((bf16[256,640]{1,0:T(8,128)(2,1)}, bf16[256,640]{1,0:T(8,128)(2,1)}, u32[]{:S(2)}, u32[]{:S(2)}) %collective-permute-start.25) | collective-permute-done | bytes 327712 | tf_op jit(solution)/shard_map/ppermute | solution.py:39
  167.3 9.0 %collective-permute-done.27 = bf16[256,640]{1,0:T(8,128)(2,1)} collective-permute-done((bf16[256,640]{1,0:T(8,128)(2,1)}, bf16[256,640]{1,0:T(8,128)(2,1)}, u32[]{:S(2)}, u32[]{:S(2)}) %collective-permute-start.27) | collective-permute-done | bytes 327712 | tf_op jit(solution)/shard_map/ppermute | solution.py:39
  181.1 4.8 %ffn_weights_here.3 = (bf16[640,1280]{1,0:T(8,128)(2,1)}, bf16[2,640,640]{2,1,0:T(8,128)(2,1)}) custom-call(s32[1]{0:T(128)} %bitcast.11.place_ref, bf16[2,640,1280]{2,1,0:T(8,128)(2,1)} %up_home_ref.3, bf16[2,2,640,640]{3,2,1,0:T(8,128)(2,1)} %bitcast.159, bf16[4,320,640]{2,1,0:T(8,128)(2,1)} %copy-done.12), custom_call_target="tpu_custom_call" | custom-call | flops 4600000000 | bytes 1048576 | tf_op jit(solution)/shard_map/ffn_weights_here/pallas_call | solution.py:181
  214.8 4.8 %all-to-all-start.3 = ((bf16[4,640,640]{2,1,0:T(8,128)(2,1)}), bf16[4,640,640]{2,1,0:T(8,128)(2,1)}, u32[]{:S(2)}, u32[]{:S(2)}) async-start(bf16[4,640,640]{2,1,0:T(8,128)(2,1)} %pad_maximum_fusion), calls=%async_computation.3 | async-start | bytes 6553600 | tf_op jit(solution)/shard_map/all_to_all | solution.py:152
  227.6 5.7 %collective-permute-done.36.refs_6_ = bf16[256,640]{1,0:T(8,128)(2,1)S(1)} collective-permute-done((bf16[256,640]{1,0:T(8,128)(2,1)}, bf16[256,640]{1,0:T(8,128)(2,1)S(1)}, u32[]{:S(2)}, u32[]{:S(2)}) %collective-permute-start.36) | collective-permute-done | bytes 327712 | tf_op jit(solution)/shard_map/ppermute | solution.py:39
  238.3 20.6 %attend_backward.2 = (bf16[256,640]{1,0:T(8,128)(2,1)}, bf16[256,640]{1,0:T(8,128)(2,1)}, bf16[256,640]{1,0:T(8,128)(2,1)}, bf16[256,640]{1,0:T(8,128)(2,1)}, bf...) custom-call(bf16[1024,480]{1,0:T(8,128)(2,1)} %get-tuple-element.233.refs_0_, f32[1024,1024]{1,0:T(8,128)} %fusion.1.bias_ref.refs_1_, ...), custom_call_target="tpu_custom_call" | custom-call | flops 6899999744 | bytes 1048576 | tf_op jit(solution)/shard_map/attend_backward/pallas_call | solution.py:454
  266.0 4.4 all-to-all-start.4
  279.4 5.4 %collective-permute-done.46 = bf16[256,640]{1,0:T(8,128)(2,1)S(1)} collective-permute-done((bf16[256,640]{1,0:T(8,128)(2,1)}, bf16[256,640]{1,0:T(8,128)(2,1)S(1)}, u32[]{:S(2)}, u32[]{:S(2)}) %collective-permute-start.46) | collective-permute-done | bytes 327712 | tf_op jit(solution)/shard_map/ppermute | solution.py:39
  302.5 4.1 all-to-all-start.5
  314.2 4.6 collective-permute-done.52.refs_6_
  324.0 20.6 %attend_backward.3 = (bf16[256,640]{1,0:T(8,128)(2,1)}, bf16[256,640]{1,0:T(8,128)(2,1)}, bf16[256,640]{1,0:T(8,128)(2,1)}, bf16[256,640]{1,0:T(8,128)(2,1)}, bf...) custom-call(bf16[1024,480]{1,0:T(8,128)(2,1)} %get-tuple-element.273.refs_0_, f32[1024,1024]{1,0:T(8,128)} %fusion.1.bias_ref.refs_1_, ...), custom_call_target="tpu_custom_call" | custom-call | flops 6899999744 | bytes 1048576 | tf_op jit(solution)/shard_map/attend_backward/pallas_call | solution.py:454
  344.6 6.7 %collective-permute-done.50 = bf16[480,640]{1,0:T(8,128)(2,1)} collective-permute-done((bf16[480,640]{1,0:T(8,128)(2,1)S(1)}, bf16[480,640]{1,0:T(8,128)(2,1)}, u32[]{:S(2)}, u32[]{:S(2)}) %collective-permute-start.50) | collective-permute-done | bytes 614432 | tf_op jit(solution)/shard_map/ppermute | solution.py:39
  365.1 6.6 %collective-permute-done.56.plane_ref = bf16[256,640]{1,0:T(8,128)(2,1)} collective-permute-done((bf16[256,640]{1,0:T(8,128)(2,1)}, bf16[256,640]{1,0:T(8,128)(2,1)}, u32[]{:S(2)}, u32[]{:S(2)}) %collective-permute-start.56) | collective-permute-done | bytes 327712 | tf_op jit(solution)/shard_map/ppermute | solution.py:39
  371.6 5.9 %collective-permute-done.57 = bf16[320,640]{1,0:T(8,128)(2,1)S(1)} collective-permute-done((bf16[320,640]{1,0:T(8,128)(2,1)S(1)}, bf16[320,640]{1,0:T(8,128)(2,1)S(1)}, u32[]{:S(2)}, u32[]{:S(2)}) %collective-permute-start.57) | collective-permute-done | bytes 409632 | tf_op jit(solution)/shard_map/ppermute | solution.py:39
  383.0 4.0 all-to-all-start.7
  391.5 8.9 %collective-permute-done.59 = bf16[192,640]{1,0:T(8,128)(2,1)S(1)} collective-permute-done((bf16[192,640]{1,0:T(8,128)(2,1)S(1)}, bf16[192,640]{1,0:T(8,128)(2,1)S(1)}, u32[]{:S(2)}, u32[]{:S(2)}) %collective-permute-start.59) | collective-permute-done | bytes 245792 | tf_op jit(solution)/shard_map/ppermute | solution.py:39
  400.6 5.8 %all-to-all-done.7.mine_ref = bf16[4,320,640]{2,1,0:T(8,128)(2,1)S(1)} async-done(((bf16[4,320,640]{2,1,0:T(8,128)(2,1)}), bf16[4,320,640]{2,1,0:T(8,128)(2,1)S(1)}, u32[]{:S(2)}, u32[]{:S(2)}) %all-to-all-start.7) | async-done | bytes 1638432 | tf_op jit(solution)/shard_map/all_to_all | solution.py:152
  424.4 5.1 %ffn_grads.2 = (f32[2,640,1280]{2,1,0:T(8,128)}, f32[2,2,640,640]{3,2,1,0:T(8,128)}) custom-call(s32[1]{0:T(128)} %bitcast.11.place_ref, bf16[4,320,640]{2,1,0:T(8,128)(2,1)} %copy-done.10, bf16[4,320,640]{2,1,0:T(8,128)(2,1)} %collective-permute-done.60.other_ref), custom_call_target="tpu_custom_call" | custom-call | flops 4600000000 | bytes 1048576 | tf_op jit(solution)/shard_map/ffn_grads/pallas_call | solution.py:225
  429.6 21.7 %all-to-all-done.8.mine_ref = bf16[4,672,640]{2,1,0:T(8,128)(2,1)S(1)} async-done(((bf16[4,672,640]{2,1,0:T(8,128)(2,1)}), bf16[4,672,640]{2,1,0:T(8,128)(2,1)S(1)}, u32[]{:S(2)}, u32[]{:S(2)}) %all-to-all-start.8) | async-done | bytes 3440672 | tf_op jit(solution)/shard_map/all_to_all | solution.py:152
  453.4 4.0 collective-permute-done.63.other_ref
  463.7 5.1 %ffn_grads.3 = (f32[2,640,1280]{2,1,0:T(8,128)}, f32[2,2,640,640]{3,2,1,0:T(8,128)}) custom-call(s32[1]{0:T(128)} %bitcast.11.place_ref, bf16[4,672,640]{2,1,0:T(8,128)(2,1)} %copy-done.3, bf16[4,672,640]{2,1,0:T(8,128)(2,1)} %copy-done.4, f32[2,640,1280]{2,1,0:T(8,128)} %get-tuple-element.313.refs_0_, ...), custom_call_target="tpu_custom_call", output_to_operand_aliasing={{0}: (3, {}), {1}: (4, {})} | custom-call | flops 4600000000 | bytes 1048576 | tf_op jit(solution)/shard_map/ffn_grads/pallas_call | solution.py:225
  (390 shorter events, 230.1 us)
Async XLA Ops:
  5.2 35.8 %collective-permute-start.6 = (bf16[160,640]{1,0:T(8,128)(2,1)S(1)}, bf16[160,640]{1,0:T(8,128)(2,1)S(1)}, u32[]{:S(2)}, u32[]{:S(2)}) collective-permute-start(bf16[160,640]{1,0:T(8,128)(2,1)S(1)} %get-tuple-element.339), channel_id=1, source_target_pairs={{0,0},{1,1},{2,4},{3,5},{4,2},{5,3},{6,6},{7,7},{8,8},{9,9},{10,12... | collective-permute-start | bytes 614408 | tf_op jit(solution)/shard_map/ppermute | solution.py:35
  7.3 33.7 %collective-permute-start.5 = (bf16[480,640]{1,0:T(8,128)(2,1)S(1)}, bf16[480,640]{1,0:T(8,128)(2,1)}, u32[]{:S(2)}, u32[]{:S(2)}) collective-permute-start(bf16[480,640]{1,0:T(8,128)(2,1)S(1)} %bitcast.161), channel_id=1, source_target_pairs={{0,0},{1,1},{2,4},{3,5},{4,2},{5,3},{6,6},{7,7},{8,8},{9,9},{10,12... | collective-permute-start | bytes 1843208 | tf_op jit(solution)/shard_map/ppermute | solution.py:35
  18.9 22.1 %collective-permute-start.2 = (bf16[256,640]{1,0:T(8,128)(2,1)}, bf16[256,640]{1,0:T(8,128)(2,1)}, u32[]{:S(2)}, u32[]{:S(2)}) collective-permute-start(bf16[256,640]{1,0:T(8,128)(2,1)} %get-tuple-element.168.own_x_ref), channel_id=1, source_target_pairs={{0,4},{4,0},{1,5},{5,1},{2,6},{6,2},{3,7},{7,3},{8,12},{12,8},{9,1... | collective-permute-start | bytes 983048 | tf_op jit(solution)/shard_map/ppermute | solution.py:39
  25.9 15.1 %collective-permute-start.4 = (bf16[256,640]{1,0:T(8,128)(2,1)}, bf16[256,640]{1,0:T(8,128)(2,1)}, u32[]{:S(2)}, u32[]{:S(2)}) collective-permute-start(bf16[256,640]{1,0:T(8,128)(2,1)} %collective-permute-done.3.plane_x_ref), channel_id=1, source_target_pairs={{0,4},{4,0},{1,5},{5,1},{2,6},{6,2},{3,7},{7,3},{8,12},{12,8},{9,1... | collective-permute-start | bytes 983048 | tf_op jit(solution)/shard_map/ppermute | solution.py:39
  37.8 22.1 %collective-permute-start.7 = (bf16[320,640]{1,0:T(8,128)(2,1)S(1)}, bf16[320,640]{1,0:T(8,128)(2,1)S(1)}, u32[]{:S(2)}, u32[]{:S(2)}) collective-permute-start(bf16[320,640]{1,0:T(8,128)(2,1)S(1)} %pad_maximum_fusion.7), channel_id=1, source_target_pairs={{0,2},{2,0},{1,3},{3,1},{4,6},{6,4},{5,7},{7,5},{8,10},{10,8},{9,1... | collective-permute-start | bytes 1228808 | tf_op jit(solution)/shard_map/ppermute | solution.py:39
  64.9 23.8 %all-to-all-start = ((bf16[4,320,640]{2,1,0:T(8,128)(2,1)}), bf16[4,320,640]{2,1,0:T(8,128)(2,1)S(1)}, u32[]{:S(2)}, u32[]{:S(2)}) async-start(bf16[4,320,640]{2,1,0:T(8,128)(2,1)} %broadcast_in_dim.32), calls=%async_computation | async-start | bytes 3276800 | tf_op jit(solution)/shard_map/all_to_all | solution.py:152
  77.5 23.5 %collective-permute-start.16 = (bf16[256,640]{1,0:T(8,128)(2,1)}, bf16[256,640]{1,0:T(8,128)(2,1)}, u32[]{:S(2)}, u32[]{:S(2)}) collective-permute-start(bf16[256,640]{1,0:T(8,128)(2,1)} %param.23), channel_id=1, source_target_pairs={{0,0},{1,1},{2,4},{3,5},{4,2},{5,3},{6,6},{7,7},{8,8},{9,9},{10,12... | collective-permute-start | bytes 983048 | tf_op jit(solution)/shard_map/ppermute | solution.py:35
  81.5 19.4 %collective-permute-start.15 = (bf16[160,640]{1,0:T(8,128)(2,1)}, bf16[160,640]{1,0:T(8,128)(2,1)S(1)}, u32[]{:S(2)}, u32[]{:S(2)}) collective-permute-start(bf16[160,640]{1,0:T(8,128)(2,1)} %fusion.101), channel_id=1, source_target_pairs={{0,2},{2,0},{1,3},{3,1},{4,6},{6,4},{5,7},{7,5},{8,10},{10,8},{9,1... | collective-permute-start | bytes 614408 | tf_op jit(solution)/shard_map/ppermute | solution.py:39
  111.1 15.1 %all-to-all-start.1 = ((bf16[4,160,640]{2,1,0:T(8,128)(2,1)}), bf16[4,160,640]{2,1,0:T(8,128)(2,1)S(1)}, u32[]{:S(2)}, u32[]{:S(2)}) async-start(bf16[4,160,640]{2,1,0:T(8,128)(2,1)} %broadcast_in_dim.33), calls=%async_computation.1 | async-start | bytes 1638400 | tf_op jit(solution)/shard_map/all_to_all | solution.py:152
  128.9 21.6 %collective-permute-start.22 = (bf16[320,640]{1,0:T(8,128)(2,1)S(1)}, bf16[320,640]{1,0:T(8,128)(2,1)S(1)}, u32[]{:S(2)}, u32[]{:S(2)}) collective-permute-start(bf16[320,640]{1,0:T(8,128)(2,1)S(1)} %copy-done.30), channel_id=1, source_target_pairs={{0,2},{2,0},{1,3},{3,1},{4,6},{6,4},{5,7},{7,5},{8,10},{10,8},{9,1... | collective-permute-start | bytes 1228808 | tf_op jit(solution)/shard_map/ppermute | solution.py:39
  156.0 23.9 %all-to-all-start.2 = ((bf16[4,320,640]{2,1,0:T(8,128)(2,1)}), bf16[4,320,640]{2,1,0:T(8,128)(2,1)S(1)}, u32[]{:S(2)}, u32[]{:S(2)}) async-start(bf16[4,320,640]{2,1,0:T(8,128)(2,1)} %broadcast_in_dim.34), calls=%async_computation.2 | async-start | bytes 3276800 | tf_op jit(solution)/shard_map/all_to_all | solution.py:152
  167.3 18.6 %collective-permute-start.26 = (bf16[256,640]{1,0:T(8,128)(2,1)}, bf16[256,640]{1,0:T(8,128)(2,1)}, u32[]{:S(2)}, u32[]{:S(2)}) collective-permute-start(bf16[256,640]{1,0:T(8,128)(2,1)} %get-tuple-element.225), channel_id=1, source_target_pairs={{0,4},{4,0},{1,5},{5,1},{2,6},{6,2},{3,7},{7,3},{8,12},{12,8},{9,1... | collective-permute-start | bytes 983048 | tf_op jit(solution)/shard_map/ppermute | solution.py:39
  186.0 12.5 %collective-permute-start.32 = (bf16[256,640]{1,0:T(8,128)(2,1)}, bf16[256,640]{1,0:T(8,128)(2,1)S(1)}, u32[]{:S(2)}, u32[]{:S(2)}) collective-permute-start(bf16[256,640]{1,0:T(8,128)(2,1)} %collective-permute-done.16.grad_ref), channel_id=1, source_target_pairs={{0,4},{4,0},{1,5},{5,1},{2,6},{6,2},{3,7},{7,3},{8,12},{12,8},{9,1... | collective-permute-start | bytes 983048 | tf_op jit(solution)/shard_map/ppermute | solution.py:39
  186.0 12.2 %collective-permute-start.29 = (bf16[256,640]{1,0:T(8,128)(2,1)}, bf16[256,640]{1,0:T(8,128)(2,1)S(1)}, u32[]{:S(2)}, u32[]{:S(2)}) collective-permute-start(bf16[256,640]{1,0:T(8,128)(2,1)} %collective-permute-done.16.grad_ref), channel_id=1, source_target_pairs={{0,1},{1,0},{2,3},{3,2},{4,5},{5,4},{6,7},{7,6},{8,9},{9,8},{10,11... | collective-permute-start | bytes 983048 | tf_op jit(solution)/shard_map/ppermute | solution.py:39
  200.8 18.9 %collective-permute-start.33 = (bf16[256,640]{1,0:T(8,128)(2,1)}, bf16[256,640]{1,0:T(8,128)(2,1)S(1)}, u32[]{:S(2)}, u32[]{:S(2)}) collective-permute-start(bf16[256,640]{1,0:T(8,128)(2,1)} %convolution_convert_fusion.14), channel_id=1, source_target_pairs={{0,4},{4,0},{1,5},{5,1},{2,6},{6,2},{3,7},{7,3},{8,12},{12,8},{9,1... | collective-permute-start | bytes 983048 | tf_op jit(solution)/shard_map/ppermute | solution.py:39
  205.8 13.9 %collective-permute-start.34 = (bf16[256,640]{1,0:T(8,128)(2,1)}, bf16[256,640]{1,0:T(8,128)(2,1)}, u32[]{:S(2)}, u32[]{:S(2)}) collective-permute-start(bf16[256,640]{1,0:T(8,128)(2,1)} %add_convert_fusion.6), channel_id=1, source_target_pairs={{0,1},{1,0},{2,3},{3,2},{4,5},{5,4},{6,7},{7,6},{8,9},{9,8},{10,11... | collective-permute-start | bytes 983048 | tf_op jit(solution)/shard_map/ppermute | solution.py:39
  214.8 44.1 %all-to-all-start.3 = ((bf16[4,640,640]{2,1,0:T(8,128)(2,1)}), bf16[4,640,640]{2,1,0:T(8,128)(2,1)}, u32[]{:S(2)}, u32[]{:S(2)}) async-start(bf16[4,640,640]{2,1,0:T(8,128)(2,1)} %pad_maximum_fusion), calls=%async_computation.3 | async-start | bytes 6553600 | tf_op jit(solution)/shard_map/all_to_all | solution.py:152
  235.3 23.7 %collective-permute-start.40 = (bf16[256,640]{1,0:T(8,128)(2,1)S(1)}, bf16[256,640]{1,0:T(8,128)(2,1)}, u32[]{:S(2)}, u32[]{:S(2)}) collective-permute-start(bf16[256,640]{1,0:T(8,128)(2,1)S(1)} %convolution_convert_fusion.12), channel_id=1, source_target_pairs={{0,4},{4,0},{1,5},{5,1},{2,6},{6,2},{3,7},{7,3},{8,12},{12,8},{9,1... | collective-permute-start | bytes 983048 | tf_op jit(solution)/shard_map/ppermute | solution.py:39
  236.6 22.4 %collective-permute-start.39 = (bf16[256,640]{1,0:T(8,128)(2,1)S(1)}, bf16[256,640]{1,0:T(8,128)(2,1)}, u32[]{:S(2)}, u32[]{:S(2)}) collective-permute-start(bf16[256,640]{1,0:T(8,128)(2,1)S(1)} %add_convert_fusion.5), channel_id=1, source_target_pairs={{0,1},{1,0},{2,3},{3,2},{4,5},{5,4},{6,7},{7,6},{8,9},{9,8},{10,11... | collective-permute-start | bytes 983048 | tf_op jit(solution)/shard_map/ppermute | solution.py:39
  266.0 31.9 %all-to-all-start.4 = ((bf16[4,160,640]{2,1,0:T(8,128)(2,1)}), bf16[4,160,640]{2,1,0:T(8,128)(2,1)}, u32[]{:S(2)}, u32[]{:S(2)}) async-start(bf16[4,160,640]{2,1,0:T(8,128)(2,1)} %bitcast.33), calls=%async_computation.4 | async-start | bytes 1638400 | tf_op jit(solution)/shard_map/all_to_all | solution.py:152
  287.1 13.9 %collective-permute-start.45 = (bf16[256,640]{1,0:T(8,128)(2,1)}, bf16[256,640]{1,0:T(8,128)(2,1)}, u32[]{:S(2)}, u32[]{:S(2)}) collective-permute-start(bf16[256,640]{1,0:T(8,128)(2,1)} %convolution_convert_fusion.8), channel_id=1, source_target_pairs={{0,4},{4,0},{1,5},{5,1},{2,6},{6,2},{3,7},{7,3},{8,12},{12,8},{9,1... | collective-permute-start | bytes 983048 | tf_op jit(solution)/shard_map/ppermute | solution.py:39
  302.5 48.9 %all-to-all-start.5 = ((bf16[4,640,640]{2,1,0:T(8,128)(2,1)}), bf16[4,640,640]{2,1,0:T(8,128)(2,1)S(1)}, u32[]{:S(2)}, u32[]{:S(2)}) async-start(bf16[4,640,640]{2,1,0:T(8,128)(2,1)} %pad_maximum_fusion.1), calls=%async_computation.5 | async-start | bytes 6553600 | tf_op jit(solution)/shard_map/all_to_all | solution.py:152
  310.6 12.6 %collective-permute-start.51 = (bf16[256,640]{1,0:T(8,128)(2,1)}, bf16[256,640]{1,0:T(8,128)(2,1)}, u32[]{:S(2)}, u32[]{:S(2)}) collective-permute-start(bf16[256,640]{1,0:T(8,128)(2,1)} %get-tuple-element.270.refs_4_), channel_id=1, source_target_pairs={{0,4},{4,0},{1,5},{5,1},{2,6},{6,2},{3,7},{7,3},{8,12},{12,8},{9,1... | collective-permute-start | bytes 983048 | tf_op jit(solution)/shard_map/ppermute | solution.py:39
  320.8 30.5 %collective-permute-start.50 = (bf16[480,640]{1,0:T(8,128)(2,1)S(1)}, bf16[480,640]{1,0:T(8,128)(2,1)}, u32[]{:S(2)}, u32[]{:S(2)}) collective-permute-start(bf16[480,640]{1,0:T(8,128)(2,1)S(1)} %pad_maximum_fusion.5), channel_id=1, source_target_pairs={{0,2},{2,0},{1,3},{3,1},{4,6},{6,4},{5,7},{7,5},{8,10},{10,8},{9,1... | collective-permute-start | bytes 1843208 | tf_op jit(solution)/shard_map/ppermute | solution.py:39
  352.5 12.5 %collective-permute-start.55 = (bf16[256,640]{1,0:T(8,128)(2,1)}, bf16[256,640]{1,0:T(8,128)(2,1)}, u32[]{:S(2)}, u32[]{:S(2)}) collective-permute-start(bf16[256,640]{1,0:T(8,128)(2,1)} %get-tuple-element.291), channel_id=1, source_target_pairs={{0,4},{4,0},{1,5},{5,1},{2,6},{6,2},{3,7},{7,3},{8,12},{12,8},{9,1... | collective-permute-start | bytes 983048 | tf_op jit(solution)/shard_map/ppermute | solution.py:39
  355.2 16.5 %collective-permute-start.56 = (bf16[256,640]{1,0:T(8,128)(2,1)}, bf16[256,640]{1,0:T(8,128)(2,1)}, u32[]{:S(2)}, u32[]{:S(2)}) collective-permute-start(bf16[256,640]{1,0:T(8,128)(2,1)} %add_convert_fusion.2), channel_id=1, source_target_pairs={{0,1},{1,0},{2,3},{3,2},{4,5},{5,4},{6,7},{7,6},{8,9},{9,8},{10,11... | collective-permute-start | bytes 983048 | tf_op jit(solution)/shard_map/ppermute | solution.py:39
  355.7 21.8 %collective-permute-start.57 = (bf16[320,640]{1,0:T(8,128)(2,1)S(1)}, bf16[320,640]{1,0:T(8,128)(2,1)S(1)}, u32[]{:S(2)}, u32[]{:S(2)}) collective-permute-start(bf16[320,640]{1,0:T(8,128)(2,1)S(1)} %slice.264), channel_id=1, source_target_pairs={{0,2},{2,0},{1,3},{3,1},{4,6},{6,4},{5,7},{7,5},{8,10},{10,8},{9,1... | collective-permute-start | bytes 1228808 | tf_op jit(solution)/shard_map/ppermute | solution.py:39
  361.2 20.5 %all-to-all-start.6 = ((bf16[4,160,640]{2,1,0:T(8,128)(2,1)}), bf16[4,160,640]{2,1,0:T(8,128)(2,1)S(1)}, u32[]{:S(2)}, u32[]{:S(2)}) async-start(bf16[4,160,640]{2,1,0:T(8,128)(2,1)} %bitcast.34), calls=%async_computation.6 | async-start | bytes 1638400 | tf_op jit(solution)/shard_map/all_to_all | solution.py:152
  383.0 23.4 %all-to-all-start.7 = ((bf16[4,320,640]{2,1,0:T(8,128)(2,1)}), bf16[4,320,640]{2,1,0:T(8,128)(2,1)S(1)}, u32[]{:S(2)}, u32[]{:S(2)}) async-start(bf16[4,320,640]{2,1,0:T(8,128)(2,1)} %broadcast_in_dim.70), calls=%async_computation.7 | async-start | bytes 3276800 | tf_op jit(solution)/shard_map/all_to_all | solution.py:152
  387.3 13.1 %collective-permute-start.59 = (bf16[192,640]{1,0:T(8,128)(2,1)S(1)}, bf16[192,640]{1,0:T(8,128)(2,1)S(1)}, u32[]{:S(2)}, u32[]{:S(2)}) collective-permute-start(bf16[192,640]{1,0:T(8,128)(2,1)S(1)} %pad_maximum_fusion.9), channel_id=1, source_target_pairs={{0,2},{2,0},{1,3},{3,1},{4,6},{6,4},{5,7},{7,5},{8,10},{10,8},{9,1... | collective-permute-start | bytes 737288 | tf_op jit(solution)/shard_map/ppermute | solution.py:39
  408.8 42.4 %all-to-all-start.8 = ((bf16[4,672,640]{2,1,0:T(8,128)(2,1)}), bf16[4,672,640]{2,1,0:T(8,128)(2,1)S(1)}, u32[]{:S(2)}, u32[]{:S(2)}) async-start(bf16[4,672,640]{2,1,0:T(8,128)(2,1)} %broadcast_in_dim.71), calls=%async_computation.8 | async-start | bytes 6881280 | tf_op jit(solution)/shard_map/all_to_all | solution.py:152
  412.6 11.9 %collective-permute-start.60 = (bf16[4,320,640]{2,1,0:T(8,128)(2,1)}, bf16[4,320,640]{2,1,0:T(8,128)(2,1)}, u32[]{:S(2)}, u32[]{:S(2)}) collective-permute-start(bf16[4,320,640]{2,1,0:T(8,128)(2,1)} %copy-done.10), channel_id=1, source_target_pairs={{0,4},{4,0},{1,5},{5,1},{2,6},{6,2},{3,7},{7,3},{8,12},{12,8},{9,1... | collective-permute-start | bytes 4915208 | tf_op jit(solution)/shard_map/ppermute | solution.py:39
  (108 other events, 961.7 us)
